TPU v7x, 32 devices: a whole 2x2x4 slice. The times are simulated.
32 devices in a mesh: dp: 8 (over z, y), row: 2 (over core), col: 2 (over x).
Axes of the slice: x: 2, y: 2, z: 4, core: 2. Of those that a mesh axis runs over, the one named last changes fastest.
Arguments:
- tokens: bfloat16 [32768, 768], P(('dp', 'col'), 'row'), may hold values from -6 to 6
- w_query: float32 [768, 768], P('row', 'col'), may hold values from -0.21875 to 0.21875
- w_key: float32 [768, 768], P('row', 'col'), may hold values from -0.21875 to 0.21875
- w_value: float32 [768, 768], P('row', 'col'), may hold values from -0.21875 to 0.21875
- w_attn_out: float32 [768, 768], P('col', 'row'), may hold values from -0.875 to 0.875
- w_inter: float32 [768, 3072], P('row', 'col'), may hold values from -0.21875 to 0.21875
- w_ffout: float32 [3072, 768], P('col', 'row'), may hold values from -0.109375 to 0.109375
- b_query: float32 [768], replicated, may hold values from -3 to 3
- b_value: float32 [768], replicated, may hold values from -3 to 3
- b_attn_out: float32 [768], replicated, may hold values from -3 to 3
- b_inter: float32 [3072], replicated, may hold values from -3 to 3
- b_ffout: float32 [768], replicated, may hold values from -3 to 3
- gain_one: float32 [768], replicated, may hold values from 0.25 to 1.75
- shift_one: float32 [768], replicated, may hold values from -3 to 3
- gain_two: float32 [768], replicated, may hold values from 0.25 to 1.75
- shift_two: float32 [768], replicated, may hold values from -3 to 3
- lengths: int32 [16], replicated, may hold values from 1025 to 2048, as said below
- block_order: int32 [12, 2], replicated, may hold values from 0 to 1, each once within a row
- cotangent: bfloat16 [32768, 768], P(('dp', 'col'), 'row'), may hold values from -6 to 6
Outputs:
- layer_out: bfloat16 [32768, 768], P(('dp', 'col'), 'row')
- grad_tokens: float32 [32768, 768], P(('dp', 'col'), 'row')
- grad_w_query: float32 [768, 768], P('row', 'col')
- grad_w_key: float32 [768, 768], P('row', 'col')
- grad_w_value: float32 [768, 768], P('row', 'col')
- grad_w_attn_out: float32 [768, 768], P('col', 'row')
- grad_w_inter: float32 [768, 3072], P('row', 'col')
- grad_w_ffout: float32 [3072, 768], P('col', 'row')
- grad_b_query: float32 [768], replicated
- grad_b_value: float32 [768], replicated
- grad_b_attn_out: float32 [768], replicated
- grad_b_inter: float32 [3072], replicated
- grad_b_ffout: float32 [768], replicated
- grad_gain_one: float32 [768], replicated
- grad_shift_one: float32 [768], replicated
- grad_gain_two: float32 [768], replicated
- grad_shift_two: float32 [768], replicated
Inputs may be any that keep to these rules, and one draw needn't show every extreme that they name: `lengths`: every sequence is longer than half of 2048; one sequence fills all 2048 slots. `block_order`: each row holds 0 and 1 once each.
All inputs are finite; a program needn't handle non-finite values.
Results may differ from a plain program's by a relative error of at most 0.02.
Values may be sent and summed in bfloat16 or wider, within the bound.
No kernel may reach another device: no remote copies, remote signals or barrier semaphores. Data moves between devices by JAX's collectives and lax.ppermute only.
A program may use at most 192 MiB of HBM per device.

v0:
```python
import jax
import jax.numpy as jnp
from jax import lax
from jax.sharding import PartitionSpec as P

D = 768
HD = 64
FF = 3072
SEQ = 2048


eps_norm = 1e-05
masked_score = -1e30


def product(left, right):
    return jnp.dot(left, right, preferred_element_type=jnp.float32)


def transposed(left, right):
    return lax.dot_general(
        left, right, (((1,), (1,)), ((), ())), preferred_element_type=jnp.float32
    )


def outer_sum(left, right):
    return lax.dot_general(
        left, right, (((0,), (0,)), ((), ())), preferred_element_type=jnp.float32
    )


def gelu_exact(values):
    return jax.nn.gelu(values, approximate=False)


def placed(values, start, total):
    return lax.dynamic_update_slice(jnp.zeros((total,), jnp.float32), values, (start,))


def gather_cols(values):
    return lax.all_gather(values, "col", axis=0, tiled=True)


def gather_rows(values):
    return lax.all_gather(values, "row", axis=0, tiled=True)


def sum_rows(values):
    return lax.psum_scatter(values, "row", scatter_dimension=0, tiled=True)


def sum_cols(values):
    return lax.psum_scatter(
        values.astype(jnp.bfloat16), "col", scatter_dimension=0, tiled=True
    ).astype(jnp.float32)


def shared_sums(total_one, total_two):
    return lax.psum((total_one, total_two), "row")


def norm_forward(values, gain, shift, reducer):
    total, squares = reducer(jnp.sum(values, 1), jnp.sum(values * values, 1))
    mean = total / D
    variance = squares / D - mean * mean
    scale = lax.rsqrt(variance + eps_norm)
    normal = (values - mean[:, None]) * scale[:, None]
    return (normal * gain + shift, normal, scale)


def norm_backward(grad, normal, scale, gain, reducer):
    inner = grad * gain
    sum_plain, sum_normal = reducer(jnp.sum(inner, 1), jnp.sum(inner * normal, 1))
    return scale[:, None] * (inner - sum_plain[:, None] / D - normal * (sum_normal / D)[:, None])


def head_block(
    query, key_all, value_all, orders, lengths_here, index, heads_local, parts, my_part, seq_rows
):
    half = SEQ // 2
    per_seq = heads_local * parts
    seq_index = index // per_seq
    head = index % per_seq // parts
    offset = index % parts
    part = offset + my_part
    source = orders[head, part]
    query_row = seq_index * seq_rows + offset * half
    select = source * 0
    key_row = seq_index * seq_rows + source * half
    column = head * HD
    query_block = lax.dynamic_slice(query, (query_row, column), (half, HD))
    key_block = lax.dynamic_slice(key_all, (select, key_row, column), (1, half, HD))[0]
    value_block = lax.dynamic_slice(value_all, (select, key_row, column), (1, half, HD))[0]
    positions = source * half + jnp.arange(half)
    live = positions < lengths_here[seq_index]
    scores = transposed(query_block, key_block) * HD ** (-0.5)
    scores = jnp.where(live[None, :], scores, masked_score)
    return (query_row, key_row, select, column, head, query_block, key_block, value_block, scores)


def attend_forward(query, key_all, value_all, orders, lengths_here, parts, my_part, seq_rows):
    rows, width = query.shape
    heads_local = width // HD
    count = rows // seq_rows * heads_local * parts

    def step(index, carry):
        blended_attention_output, logsum = carry
        query_row, key_row, select, column, head, query_block, key_block, value_block, scores = (
            head_block(
                query,
                key_all,
                value_all,
                orders,
                lengths_here,
                index,
                heads_local,
                parts,
                my_part,
                seq_rows,
            )
        )
        top = jnp.max(scores, 1, keepdims=True)
        expo = jnp.exp(scores - top)
        total = jnp.sum(expo, 1, keepdims=True)
        attention_probabilities = (expo / total).astype(jnp.bfloat16)
        blended_attention_output = lax.dynamic_update_slice(
            blended_attention_output,
            product(attention_probabilities, value_block),
            (query_row, column),
        )
        logsum = lax.dynamic_update_slice(logsum, top + jnp.log(total), (query_row, head))
        return (blended_attention_output, logsum)

    start = (jnp.zeros((rows, width), jnp.float32), jnp.zeros((rows, heads_local), jnp.float32))
    return lax.fori_loop(0, count, step, start)


def attend_backward(
    query, key_all, value_all, grad_mixed, logsum, orders, lengths_here, parts, my_part, seq_rows
):
    rows, width = query.shape
    heads_local = width // HD
    count = rows // seq_rows * heads_local * parts
    half = SEQ // 2

    def step(index, carry):
        grad_query, grad_key, grad_value = carry
        query_row, key_row, select, column, head, query_block, key_block, value_block, scores = (
            head_block(
                query,
                key_all,
                value_all,
                orders,
                lengths_here,
                index,
                heads_local,
                parts,
                my_part,
                seq_rows,
            )
        )
        logsum_block = lax.dynamic_slice(logsum, (query_row, head), (half, 1))
        attention_probabilities = jnp.exp(scores - logsum_block)
        grad_block = lax.dynamic_slice(grad_mixed, (query_row, column), (half, HD))
        grad_probs = transposed(grad_block, value_block)
        inner = jnp.sum(grad_probs * attention_probabilities, 1, keepdims=True)
        grad_scores = (attention_probabilities * (grad_probs - inner) * HD ** (-0.5)).astype(
            jnp.bfloat16
        )
        grad_query = lax.dynamic_update_slice(
            grad_query, product(grad_scores, key_block), (query_row, column)
        )
        grad_key = lax.dynamic_update_slice(
            grad_key, outer_sum(grad_scores, query_block)[None], (select, key_row, column)
        )
        grad_value = lax.dynamic_update_slice(
            grad_value,
            outer_sum(attention_probabilities.astype(jnp.bfloat16), grad_block)[None],
            (select, key_row, column),
        )
        return (grad_query, grad_key, grad_value)

    empty_query = jnp.zeros((rows, width), jnp.float32)
    empty_keys = jnp.zeros(key_all.shape, jnp.float32)
    return lax.fori_loop(0, count, step, (empty_query, empty_keys, empty_keys))


def grid_plan(tokens, weights, vectors, lengths, block_order, cotangent):
    w_query, w_key, w_value, w_attn_out, w_inter, w_ffout = weights
    b_query, b_value, b_attn_out, b_inter, b_ffout, gain_one, shift_one, gain_two, shift_two = (
        vectors
    )
    rows_col, width_row = tokens.shape
    width_col = w_query.shape[1]
    ff_col = w_inter.shape[1]
    n_row = lax.axis_size("row")
    n_col = lax.axis_size("col")
    row_index = lax.axis_index("row")
    col_index = lax.axis_index("col")
    group_rows = rows_col * n_col
    rows_row = group_rows // n_row
    per_col = rows_col // SEQ
    per_row = rows_row // SEQ
    group_first = lax.axis_index("dp") * (group_rows // SEQ)
    lengths_col = lax.dynamic_slice(lengths, (group_first + col_index * per_col,), (per_col,))
    lengths_row = lax.dynamic_slice(lengths, (group_first + row_index * per_row,), (per_row,))
    live = (
        (jnp.arange(SEQ)[None, :] < lengths_col[:, None]).astype(jnp.float32).reshape(rows_col, 1)
    )
    heads_local = width_col // HD
    orders = lax.dynamic_slice(block_order, (col_index * heads_local, 0), (heads_local, 2))
    row_start = row_index * width_row
    col_start = col_index * width_col
    ff_start = col_index * ff_col
    b_query_here = lax.dynamic_slice_in_dim(b_query, col_start, width_col)
    b_value_here = lax.dynamic_slice_in_dim(b_value, col_start, width_col)
    b_inter_here = lax.dynamic_slice_in_dim(b_inter, ff_start, ff_col)
    b_attn_here = lax.dynamic_slice_in_dim(b_attn_out, row_start, width_row)
    b_ffout_here = lax.dynamic_slice_in_dim(b_ffout, row_start, width_row)
    gain_one_here = lax.dynamic_slice_in_dim(gain_one, row_start, width_row)
    shift_one_here = lax.dynamic_slice_in_dim(shift_one, row_start, width_row)
    gain_two_here = lax.dynamic_slice_in_dim(gain_two, row_start, width_row)
    shift_two_here = lax.dynamic_slice_in_dim(shift_two, row_start, width_row)
    qkv_w = jnp.concatenate(
        [w_query.astype(jnp.bfloat16), w_key.astype(jnp.bfloat16), w_value.astype(jnp.bfloat16)], 1
    )
    attn_w = w_attn_out.astype(jnp.bfloat16)
    inter_w = w_inter.astype(jnp.bfloat16)
    ffout_w = w_ffout.astype(jnp.bfloat16)
    whole_tokens = gather_cols(tokens)
    qkv_total = sum_rows(product(whole_tokens, qkv_w))
    query_low = (qkv_total[:, :width_col] + b_query_here).astype(jnp.bfloat16)
    key_low = qkv_total[:, width_col : 2 * width_col].astype(jnp.bfloat16)
    value_low = (qkv_total[:, 2 * width_col :] + b_value_here).astype(jnp.bfloat16)
    blended_attention_output, logsum = attend_forward(
        query_low, key_low[None], value_low[None], orders, lengths_row, 2, 0, SEQ
    )
    whole_mixed = gather_rows(blended_attention_output.astype(jnp.bfloat16))
    residual_one = tokens.astype(jnp.float32) + sum_cols(product(whole_mixed, attn_w)) + b_attn_here
    normed_one, normal_one, scale_one = norm_forward(
        residual_one, gain_one_here, shift_one_here, shared_sums
    )
    whole_normed = gather_cols(normed_one.astype(jnp.bfloat16))
    hidden_pre = sum_rows(product(whole_normed, inter_w)) + b_inter_here
    hidden, gelu_back = jax.vjp(gelu_exact, hidden_pre)
    whole_hidden = gather_rows(hidden.astype(jnp.bfloat16))
    residual_two = normed_one + sum_cols(product(whole_hidden, ffout_w)) + b_ffout_here
    layer_out, normal_two, scale_two = norm_forward(
        residual_two, gain_two_here, shift_two_here, shared_sums
    )
    grad_out = cotangent.astype(jnp.float32) * live
    grad_gain_two = jnp.sum(grad_out * normal_two, 0)
    grad_shift_two = jnp.sum(grad_out, 0)
    grad_two = norm_backward(grad_out, normal_two, scale_two, gain_two_here, shared_sums)
    grad_b_ffout = jnp.sum(grad_two, 0)
    whole_grad_two = gather_cols(grad_two.astype(jnp.bfloat16))
    grad_hidden = sum_rows(transposed(whole_grad_two, ffout_w))
    grad_w_ffout = outer_sum(whole_hidden, whole_grad_two)
    (grad_pre,) = gelu_back(grad_hidden)
    grad_pre_low = grad_pre.astype(jnp.bfloat16)
    grad_b_inter = jnp.sum(grad_pre_low.astype(jnp.float32), 0)
    whole_grad_pre = gather_rows(grad_pre_low)
    grad_w_inter = outer_sum(whole_normed, whole_grad_pre)
    grad_normed = grad_two + sum_cols(transposed(whole_grad_pre, inter_w))
    grad_gain_one = jnp.sum(grad_normed * normal_one, 0)
    grad_shift_one = jnp.sum(grad_normed, 0)
    grad_one = norm_backward(grad_normed, normal_one, scale_one, gain_one_here, shared_sums)
    grad_b_attn_out = jnp.sum(grad_one, 0)
    whole_grad_one = gather_cols(grad_one.astype(jnp.bfloat16))
    grad_mixed = sum_rows(transposed(whole_grad_one, attn_w))
    grad_w_attn_out = outer_sum(whole_mixed, whole_grad_one)
    grad_query, grad_key, grad_value = attend_backward(
        query_low,
        key_low[None],
        value_low[None],
        grad_mixed.astype(jnp.bfloat16),
        logsum,
        orders,
        lengths_row,
        2,
        0,
        SEQ,
    )
    grad_qkv_low = jnp.concatenate(
        [
            grad_query.astype(jnp.bfloat16),
            grad_key[0].astype(jnp.bfloat16),
            grad_value[0].astype(jnp.bfloat16),
        ],
        1,
    )
    grad_b_query = jnp.sum(grad_qkv_low[:, :width_col].astype(jnp.float32), 0)
    grad_b_value = jnp.sum(grad_qkv_low[:, 2 * width_col :].astype(jnp.float32), 0)
    whole_grad_qkv = gather_rows(grad_qkv_low)
    grad_tokens = grad_one + sum_cols(transposed(whole_grad_qkv, qkv_w))
    grad_qkv_w = outer_sum(whole_tokens, whole_grad_qkv)
    weight_parts = (
        grad_qkv_w[:, :width_col],
        grad_qkv_w[:, width_col : 2 * width_col],
        grad_qkv_w[:, 2 * width_col :],
        grad_w_attn_out,
        grad_w_inter,
        grad_w_ffout,
    )
    vector_parts = (
        placed(grad_b_query, col_start, D),
        placed(grad_b_value, col_start, D),
        placed(grad_b_attn_out, row_start, D),
        placed(grad_b_inter, ff_start, FF),
        placed(grad_b_ffout, row_start, D),
        placed(grad_gain_one, row_start, D),
        placed(grad_shift_one, row_start, D),
        placed(grad_gain_two, row_start, D),
        placed(grad_shift_two, row_start, D),
    )
    return (layer_out.astype(jnp.bfloat16), grad_tokens, weight_parts, vector_parts)


def per_device(
    tokens,
    w_query,
    w_key,
    w_value,
    w_attn_out,
    w_inter,
    w_ffout,
    b_query,
    b_value,
    b_attn_out,
    b_inter,
    b_ffout,
    gain_one,
    shift_one,
    gain_two,
    shift_two,
    lengths,
    block_order,
    cotangent,
):
    weights = (w_query, w_key, w_value, w_attn_out, w_inter, w_ffout)
    vectors = (
        b_query,
        b_value,
        b_attn_out,
        b_inter,
        b_ffout,
        gain_one,
        shift_one,
        gain_two,
        shift_two,
    )
    results = grid_plan(tokens, weights, vectors, lengths, block_order, cotangent)
    layer_out, grad_tokens, weight_parts, vector_parts = results
    grad_w_query, grad_w_key, grad_w_value, grad_w_attn_out, grad_w_inter, grad_w_ffout = (
        lax.psum(weight_parts[0].astype(jnp.bfloat16), "dp").astype(jnp.float32),
        lax.psum(weight_parts[1].astype(jnp.bfloat16), "dp").astype(jnp.float32),
        lax.psum(weight_parts[2].astype(jnp.bfloat16), "dp").astype(jnp.float32),
        lax.psum(weight_parts[3].astype(jnp.bfloat16), "dp").astype(jnp.float32),
        lax.psum(weight_parts[4].astype(jnp.bfloat16), "dp").astype(jnp.float32),
        lax.psum(weight_parts[5].astype(jnp.bfloat16), "dp").astype(jnp.float32),
    )
    (
        grad_b_query,
        grad_b_value,
        grad_b_attn_out,
        grad_b_inter,
        grad_b_ffout,
        grad_gain_one,
        grad_shift_one,
        grad_gain_two,
        grad_shift_two,
    ) = lax.psum(
        (
            vector_parts[0],
            vector_parts[1],
            vector_parts[2],
            vector_parts[3],
            vector_parts[4],
            vector_parts[5],
            vector_parts[6],
            vector_parts[7],
            vector_parts[8],
        ),
        ("dp", "row", "col"),
    )
    return (
        layer_out,
        grad_tokens,
        grad_w_query,
        grad_w_key,
        grad_w_value,
        grad_w_attn_out,
        grad_w_inter,
        grad_w_ffout,
        grad_b_query,
        grad_b_value,
        grad_b_attn_out,
        grad_b_inter,
        grad_b_ffout,
        grad_gain_one,
        grad_shift_one,
        grad_gain_two,
        grad_shift_two,
    )


def solution(mesh):
    return jax.shard_map(
        per_device,
        mesh=mesh,
        in_specs=(
            P(("dp", "col"), "row"),
            P("row", "col"),
            P("row", "col"),
            P("row", "col"),
            P("col", "row"),
            P("row", "col"),
            P("col", "row"),
            P(),
            P(),
            P(),
            P(),
            P(),
            P(),
            P(),
            P(),
            P(),
            P(),
            P(),
            P(("dp", "col"), "row"),
        ),
        out_specs=(
            P(("dp", "col"), "row"),
            P(("dp", "col"), "row"),
            P("row", "col"),
            P("row", "col"),
            P("row", "col"),
            P("col", "row"),
            P("row", "col"),
            P("col", "row"),
            P(),
            P(),
            P(),
            P(),
            P(),
            P(),
            P(),
            P(),
            P(),
        ),
        check_vma=False,
    )
```

profile of v0, /device:TPU:0, one launch (start us, length us, event | category | flops | bytes accessed | tf_op | source)
XLA Modules:
  0.0 1184.6 jit_solution(4707898755306142605)
XLA Ops:
  10.4 46.9 %all-gather.9.cloned.1.call-done = bf16[4096,384]{1,0:T(8,128)(2,1)} async-done(((bf16[2048,384]{1,0:T(8,128)(2,1)}), bf16[4096,384]{1,0:T(8,128)(2,1)}) %all-gather.9.cloned.1.call-update) | async-done | bytes 3145744 | tf_op jit(solution)/shard_map/all_gather | solution.py:41
  57.3 10.9 convolution_bitcast_fusion.1
  69.6 27.0 %reduce-scatter.9.cloned.1.call-done = f32[2048,1152]{0,1:T(8,128)} async-done(((f32[4096,1152]{0,1:T(8,128)}), f32[2048,1152]{0,1:T(8,128)}) %reduce-scatter.9.cloned.1.call-update) | async-done | bytes 9437200 | tf_op jit(solution)/shard_map/reduce_scatter | solution.py:49
  108.7 84.4 %while.38 = (s32[]{:T(128)}, bf16[2048,384]{0,1:T(8,128)(2,1)}, f32[2048,6]{0,1:T(8,128)S(1)}, s32[6,2]{0,1:T(2,128)S(1)}, s32[1]{0:T(128)}, /*index=5*/bf16[204...) while((s32[]{:T(128)}, bf16[2048,384]{0,1:T(8,128)(2,1)}, ...), condition=%wide.region_4.5_spmd, body=%wide.region_1.4_spmd.sunk | while | flops 281019456 | bytes 13681410 | solution.py:135
  193.2 13.5 %all-gather.11.cloned.1.call-done = bf16[4096,384]{0,1:T(8,128)(2,1)} async-done(((bf16[2048,384]{0,1:T(8,128)(2,1)}), bf16[4096,384]{0,1:T(8,128)(2,1)}) %all-gather.11.cloned.1.call-update) | async-done | bytes 3145744 | tf_op jit(solution)/shard_map/all_gather | solution.py:45
  213.5 43.8 %reduce-scatter.11.cloned.1.call-done = bf16[2048,384]{1,0:T(8,128)(2,1)} async-done(((bf16[4096,384]{1,0:T(8,128)(2,1)}), bf16[2048,384]{1,0:T(8,128)(2,1)}) %reduce-scatter.11.cloned.1.call-update) | async-done | bytes 1572880 | tf_op jit(solution)/shard_map/reduce_scatter | solution.py:53
  265.5 44.6 %all-gather.13.cloned.1.call-done = bf16[4096,384]{1,0:T(8,128)(2,1)} async-done(((bf16[2048,384]{1,0:T(8,128)(2,1)}), bf16[4096,384]{1,0:T(8,128)(2,1)}) %all-gather.13.cloned.1.call-update) | async-done | bytes 3145744 | tf_op jit(solution)/shard_map/all_gather | solution.py:41
  310.1 13.8 %fusion.62 = f32[4096,1536]{1,0:T(8,128)} fusion(bf16[4096,384]{1,0:T(8,128)(2,1)} %all-gather.13.cloned.1.call-done, f32[384,1536]{1,0:T(8,128)} %param.28), kind=kOutput, calls=%fused_computation.116 | convolution fusion | flops 4832428032 | bytes 30670848 | tf_op jit(solution)/shard_map/dot_general | solution.py:17
  324.7 34.9 %reduce-scatter.13.cloned.1.call-done = f32[2048,1536]{1,0:T(8,128)} async-done(((f32[4096,1536]{1,0:T(8,128)}), f32[2048,1536]{1,0:T(8,128)}) %reduce-scatter.13.cloned.1.call-update) | async-done | bytes 12582928 | tf_op jit(solution)/shard_map/reduce_scatter | solution.py:49
  359.5 30.2 %multiply_convert_fusion.1 = (bf16[2048,1536]{1,0:T(8,128)(2,1)}, f32[2048,1536]{1,0:T(8,128)}) fusion(f32[2048,1536]{1,0:T(8,128)} %reduce-scatter.13.cloned.1.call-done, f32[1536]{0:T(1024)S(1)} %dynamic_slice.159), kind=kLoop, calls=%fused_computation.53 | loop fusion | flops 207618048 | bytes 31463424 | tf_op jit(solution)/shard_map/convert_element_type | solution.py:246
  389.8 26.2 %all-gather.15.cloned.1.call-done = bf16[4096,1536]{1,0:T(8,128)(2,1)} async-done(((bf16[2048,1536]{1,0:T(8,128)(2,1)}), bf16[4096,1536]{1,0:T(8,128)(2,1)}) %all-gather.15.cloned.1.call-update) | async-done | bytes 12582928 | tf_op jit(solution)/shard_map/all_gather | solution.py:45
  415.9 11.5 convolution_convert_fusion.3
  429.0 43.2 %reduce-scatter.15.cloned.1.call-done = bf16[2048,384]{1,0:T(8,128)(2,1)} async-done(((bf16[4096,384]{1,0:T(8,128)(2,1)}), bf16[2048,384]{1,0:T(8,128)(2,1)}) %reduce-scatter.15.cloned.1.call-update) | async-done | bytes 1572880 | tf_op jit(solution)/shard_map/reduce_scatter | solution.py:53
  486.9 6.4 fusion.73
  493.6 44.9 %all-gather.17.cloned.1.call-done = bf16[4096,384]{1,0:T(8,128)(2,1)} async-done(((bf16[2048,384]{1,0:T(8,128)(2,1)}), bf16[4096,384]{1,0:T(8,128)(2,1)}) %all-gather.17.cloned.1.call-update) | async-done | bytes 3145744 | tf_op jit(solution)/shard_map/all_gather | solution.py:41
  538.4 13.8 %fusion.58 = f32[4096,1536]{1,0:T(8,128)} fusion(bf16[4096,384]{1,0:T(8,128)(2,1)} %all-gather.17.cloned.1.call-done, f32[1536,384]{1,0:T(8,128)} %param.29), kind=kOutput, calls=%fused_computation.112 | convolution fusion | flops 4832428032 | bytes 30670848 | tf_op jit(solution)/shard_map/dot_general | solution.py:21
  552.4 35.5 %reduce-scatter.17.cloned.1.call-done = f32[2048,1536]{1,0:T(8,128)} async-done(((f32[4096,1536]{1,0:T(8,128)}), f32[2048,1536]{1,0:T(8,128)}) %reduce-scatter.17.cloned.1.call-update) | async-done | bytes 12582928 | tf_op jit(solution)/shard_map/reduce_scatter | solution.py:49
  587.9 17.0 %convert_reduce_fusion = (f32[1536]{0:T(1024)S(1)}, bf16[2048,1536]{1,0:T(8,128)(2,1)}) fusion(f32[2048,1536]{1,0:T(8,128)} %reduce-scatter.17.cloned.1.call-done, f32[2048,1536]{1,0:T(8,128)} %get-tuple-element.691, f32[2048,1536]{1,0:T(8,128)} %reduce-scatter.13.cloned.1.call-done, f32[1536]{0:T(1024)S(1)} %dynamic_slice.159), kind=kLoop, calls=%fused_computation.51 | loop fusion | flops 53475840 | bytes 44052480 | tf_op jit(solution)/shard_map/reduce_sum | solution.py:261
  605.0 26.2 %all-gather.19.cloned.1.call-done = bf16[4096,1536]{1,0:T(8,128)(2,1)} async-done(((bf16[2048,1536]{1,0:T(8,128)(2,1)}), bf16[4096,1536]{1,0:T(8,128)(2,1)}) %all-gather.19.cloned.1.call-update) | async-done | bytes 12582928 | tf_op jit(solution)/shard_map/all_gather | solution.py:45
  631.1 11.6 convolution_convert_fusion.2
  642.8 44.6 %reduce-scatter.19.cloned.1.call-done = bf16[2048,384]{1,0:T(8,128)(2,1)} async-done(((bf16[4096,384]{1,0:T(8,128)(2,1)}), bf16[2048,384]{1,0:T(8,128)(2,1)}) %reduce-scatter.19.cloned.1.call-update) | async-done | bytes 1572880 | tf_op jit(solution)/shard_map/reduce_scatter | solution.py:53
  701.8 44.8 %all-gather.21.cloned.1.call-done = bf16[4096,384]{1,0:T(8,128)(2,1)} async-done(((bf16[2048,384]{1,0:T(8,128)(2,1)}), bf16[4096,384]{1,0:T(8,128)(2,1)}) %all-gather.21.cloned.1.call-update) | async-done | bytes 3145744 | tf_op jit(solution)/shard_map/all_gather | solution.py:41
  746.6 6.6 fusion.64
  753.2 14.6 %reduce-scatter.21.cloned.1.call-done = f32[2048,384]{1,0:T(8,128)} async-done(((f32[4096,384]{1,0:T(8,128)}), f32[2048,384]{1,0:T(8,128)}) %reduce-scatter.21.cloned.1.call-update) | async-done | bytes 3145744 | tf_op jit(solution)/shard_map/reduce_scatter | solution.py:49
  772.8 175.0 %while.39 = (s32[]{:T(128)}, bf16[2048,384]{0,1:T(8,128)(2,1)S(1)}, bf16[1,2048,384]{1,2,0:T(8,128)(2,1)}, bf16[1,2048,384]{1,2,0:T(8,128)(2,1)S(1)}, s32[6,2]{0...) while((s32[]{:T(128)}, bf16[2048,384]{0,1:T(8,128)(2,1)S(1)}, ...), condition=%wide.region_29.30_spmd, body=%wide.region_27.29_spmd.sunk | while | flops 687866944 | bytes 34122520 | solution.py:185
  951.9 11.6 convolution_convert_fusion.4
  963.4 10.5 convolution_convert_fusion.5
  976.5 8.5 fusion.54
  986.4 9.3 convolution_convert_fusion.1
  999.0 45.2 %all-reduce = (f32[768]{0:T(1024)}, f32[768]{0:T(1024)}, f32[768]{0:T(1024)}, f32[3072]{0:T(1024)}, f32[768]{0:T(1024)}, /*index=5*/f32[768]{0:T(1024)}, f32[768]{0:T(1024)}, f32[768]{0:T(1024)}, f32[768]{0:T(1024)}) all-reduce(f32[768]{0:T(1024)S(1)} %dynamic_update_slice.82, ...), channel_id=1, replica_groups=mesh['dp'=8,'row'=2,'col'=2] {'dp','row','col'}, use_global_device_ids=true, to_apply=%region_38.39 | all-reduce | flops 9216 | bytes 73728 | tf_op jit(solution)/shard_map/psum | solution.py:372
  1044.2 85.6 %all-reduce.8.cloned.1.call-done = (bf16[384,384]{0,1:T(8,128)(2,1)}, bf16[384,384]{0,1:T(8,128)(2,1)}, bf16[384,384]{0,1:T(8,128)(2,1)}, bf16[384,384]{1,0:T(8,...) async-done(((bf16[384,384]{0,1:T(8,128)(2,1)}, bf16[384,384]{0,1:T(8,128)(2,1)}, bf16[384,384]{0,1:T(8,128)(2,1)}, bf16[384,384]{1,0:T(8,128)(2,1)}, ...) | async-done | bytes 3538960 | tf_op jit(solution)/shard_map/psum | solution.py:355
  1143.6 30.6 %reduce-scatter.23.cloned.1.call-done = bf16[2048,384]{1,0:T(8,128)(2,1)} async-done(((bf16[4096,384]{1,0:T(8,128)(2,1)}), bf16[2048,384]{1,0:T(8,128)(2,1)}) %reduce-scatter.23.cloned.1.call-update) | async-done | bytes 1572880 | tf_op jit(solution)/shard_map/reduce_scatter | solution.py:53
  (358 shorter events, 337.6 us)
Async XLA Ops:
  7.2 62.4 %copy-start = (s32[12,2]{0,1:T(2,128)S(1)}, s32[12,2]{0,1:T(2,128)}, u32[]{:S(2)}) copy-start(s32[12,2]{0,1:T(2,128)} %param.40) | copy-start | bytes 292
  7.2 3.1 copy-start.15
  7.2 50.0 %all-gather.9.cloned.1.call-start = ((), (), s32[]{:S(2)}) async-start(), calls=%async_computation.8 | async-start | bytes 4718592 | tf_op jit(solution)/shard_map/all_gather | solution.py:41
  8.0 88.7 %reduce-scatter.9.cloned.1.call-start = ((), (), s32[]{:S(2)}) async-start(), calls=%async_computation.9 | async-start | bytes 28311552 | tf_op jit(solution)/shard_map/reduce_scatter | solution.py:49
  9.1 59.0 %copy-start.10 = (bf16[384,384]{1,0:T(8,128)(2,1)}, bf16[384,384]{1,0:T(8,128)(2,1)S(1)}, u32[]{:S(2)}) copy-start(bf16[384,384]{1,0:T(8,128)(2,1)S(1)} %convert_element_type.176) | copy-start | bytes 884740
  10.3 57.8 %copy-start.12 = (bf16[384,384]{1,0:T(8,128)(2,1)}, bf16[384,384]{1,0:T(8,128)(2,1)S(1)}, u32[]{:S(2)}) copy-start(bf16[384,384]{1,0:T(8,128)(2,1)S(1)} %convert_element_type.177) | copy-start | bytes 884740
  10.4 57.8 %copy-start.13 = (bf16[384,384]{1,0:T(8,128)(2,1)}, bf16[384,384]{1,0:T(8,128)(2,1)S(1)}, u32[]{:S(2)}) copy-start(bf16[384,384]{1,0:T(8,128)(2,1)S(1)} %convert_element_type.178) | copy-start | bytes 884740
  68.2 138.6 %all-gather.11.cloned.1.call-start = ((), (), s32[]{:S(2)}) async-start(), calls=%async_computation.10 | async-start | bytes 4718592 | tf_op jit(solution)/shard_map/all_gather | solution.py:45
  193.1 13.6 %copy-start.6 = (bf16[1,2048,384]{2,1,0:T(8,128)(2,1)}, bf16[1,2048,384]{2,1,0:T(8,128)(2,1)S(1)}, u32[]{:S(2)}) copy-start(bf16[1,2048,384]{2,1,0:T(8,128)(2,1)S(1)} %get-tuple-element.1001) | copy-start | bytes 4718596
  193.2 19.4 %copy-start.7 = (bf16[2048,384]{1,0:T(8,128)(2,1)}, bf16[2048,384]{1,0:T(8,128)(2,1)S(1)}, u32[]{:S(2)}) copy-start(bf16[2048,384]{1,0:T(8,128)(2,1)S(1)} %get-tuple-element.1002) | copy-start | bytes 4718596
  193.2 64.1 %reduce-scatter.11.cloned.1.call-start = ((), (), s32[]{:S(2)}) async-start(), calls=%async_computation.11 | async-start | bytes 4718592 | tf_op jit(solution)/shard_map/reduce_scatter | solution.py:53
  212.6 44.7 %copy-start.2 = (bf16[2048,384]{1,0:T(8,128)(2,1)S(1)}, bf16[2048,384]{1,0:T(8,128)(2,1)}, u32[]{:S(2)}) copy-start(bf16[2048,384]{1,0:T(8,128)(2,1)} %param.23) | copy-start | bytes 4718596
  212.6 97.5 %all-gather.13.cloned.1.call-start = ((), (), s32[]{:S(2)}) async-start(), calls=%async_computation.12 | async-start | bytes 4718592 | tf_op jit(solution)/shard_map/all_gather | solution.py:41
  257.3 5.8 copy-start.3
  265.0 94.6 %reduce-scatter.13.cloned.1.call-start = ((), (), s32[]{:S(2)}) async-start(), calls=%async_computation.13 | async-start | bytes 37748736 | tf_op jit(solution)/shard_map/reduce_scatter | solution.py:49
  323.9 92.0 %all-gather.15.cloned.1.call-start = ((), (), s32[]{:S(2)}) async-start(), calls=%async_computation.14 | async-start | bytes 18874368 | tf_op jit(solution)/shard_map/all_gather | solution.py:45
  389.7 82.4 %reduce-scatter.15.cloned.1.call-start = ((), (), s32[]{:S(2)}) async-start(), calls=%async_computation.15 | async-start | bytes 4718592 | tf_op jit(solution)/shard_map/reduce_scatter | solution.py:53
  427.5 111.0 %all-gather.17.cloned.1.call-start = ((), (), s32[]{:S(2)}) async-start(), calls=%async_computation.16 | async-start | bytes 4718592 | tf_op jit(solution)/shard_map/all_gather | solution.py:41
  493.3 94.6 %reduce-scatter.17.cloned.1.call-start = ((), (), s32[]{:S(2)}) async-start(), calls=%async_computation.17 | async-start | bytes 37748736 | tf_op jit(solution)/shard_map/reduce_scatter | solution.py:49
  552.3 78.8 %all-gather.19.cloned.1.call-start = ((), (), s32[]{:S(2)}) async-start(), calls=%async_computation.18 | async-start | bytes 18874368 | tf_op jit(solution)/shard_map/all_gather | solution.py:45
  604.9 82.5 %reduce-scatter.19.cloned.1.call-start = ((), (), s32[]{:S(2)}) async-start(), calls=%async_computation.19 | async-start | bytes 4718592 | tf_op jit(solution)/shard_map/reduce_scatter | solution.py:53
  642.7 103.9 %all-gather.21.cloned.1.call-start = ((), (), s32[]{:S(2)}) async-start(), calls=%async_computation.20 | async-start | bytes 4718592 | tf_op jit(solution)/shard_map/all_gather | solution.py:41
  700.2 46.4 %copy-start.14 = (f32[384,384]{1,0:T(8,128)S(1)}, f32[384,384]{1,0:T(8,128)}, u32[]{:S(2)}) copy-start(f32[384,384]{1,0:T(8,128)} %param.27) | copy-start | bytes 1769476
  701.5 66.3 %reduce-scatter.21.cloned.1.call-start = ((), (), s32[]{:S(2)}) async-start(), calls=%async_computation.21 | async-start | bytes 9437184 | tf_op jit(solution)/shard_map/reduce_scatter | solution.py:49
  753.2 223.3 %all-gather.23.cloned.1.call-start = ((), (), s32[]{:S(2)}) async-start(), calls=%async_computation.22 | async-start | bytes 14155776 | tf_op jit(solution)/shard_map/all_gather | solution.py:45
  951.5 178.3 %all-reduce.8.cloned.1.call-start = ((), (), s32[]{:S(2)}) async-start(), calls=%async_computation.24 | async-start | bytes 7077888 | tf_op jit(solution)/shard_map/psum | solution.py:355
  951.8 11.6 copy-start.8
  963.4 10.6 copy-start.9
  963.4 10.6 copy-start.28
  986.0 188.1 %reduce-scatter.23.cloned.1.call-start = ((), (), s32[]{:S(2)}) async-start(), calls=%async_computation.23 | async-start | bytes 4718592 | tf_op jit(solution)/shard_map/reduce_scatter | solution.py:53
  1137.5 36.7 %copy-start.5 = (f32[2048,384]{1,0:T(8,128)S(1)}, f32[2048,384]{1,0:T(8,128)}, u32[]{:S(2)}) copy-start(f32[2048,384]{1,0:T(8,128)} %copy-done.4) | copy-start | bytes 9437188
  1140.7 36.9 %copy-start.1 = (s32[12,2]{0,1:T(2,128)S(1)}, s32[12,2]{0,1:T(2,128)}, u32[]{:S(2)}) copy-start(s32[12,2]{0,1:T(2,128)} %param.40) | copy-start | bytes 292
  (14 other events, 12.1 us)
Sparse Core Ops, SparseCore 0:
  9.6 47.6 all-gather.8
  68.3 28.2 reduce-scatter.8
  193.3 13.3 all-gather.10
  212.7 44.5 reduce-scatter.10
  265.1 44.9 all-gather.12
  324.0 35.4 reduce-scatter.12
  389.8 26.0 all-gather.14
  427.6 44.5 reduce-scatter.14
  493.5 44.9 all-gather.16
  552.4 35.4 reduce-scatter.16
  605.0 26.0 all-gather.18
  642.8 44.5 reduce-scatter.18
  701.6 44.9 all-gather.20
  753.3 14.4 reduce-scatter.20
  951.7 23.0 all-gather.22
  986.2 143.6 all-reduce.7
  1132.0 42.1 reduce-scatter.22
where the time goes:
time: 1200 us; the launch traced here: 1180 us
  waiting for transfers between devices  608 us (51%)
  matrix products  291 us (24%)
  other arithmetic  148 us (12%)
  blocking collectives  58.5 us (5%)
  local copies, waits for them, and re-layouts  43.4 us (4%)
  loops' own time  18.5 us (2%)
  between operations  14.8 us (1%)
    all_gather x4, waiting for transfers between devices, gather_cols(): return lax.all_gather(values, 'col', axis=0, tiled=True)  181 us
    reduce_scatter x4, waiting for transfers between devices, sum_cols(): lax.psum_scatter(values.astype(jnp.bfloat16), 'col', scatter_dimension=0,...  162 us
    reduce_scatter x4, waiting for transfers between devices, sum_rows(): return lax.psum_scatter(values, 'row', scatter_dimension=0, tiled=True)  112 us
    dot_general x40, matrix products, transposed(): lax.dot_general(left, right, (((1,), (1,)), ((), ())), preferred_element_...  106 us
    dot_general x28, matrix products, product(): return jnp.dot(left, right, preferred_element_type=jnp.float32)  96.1 us
    dot_general x28, matrix products, outer_sum(): lax.dot_general(left, right, (((0,), (0,)), ((), ())), preferred_element_...  88.9 us
    psum x1, waiting for transfers between devices, per_device(): lax.psum(weight_parts[0].astype(jnp.bfloat16), 'dp').astype(jnp.float32)  85.6 us
    all_gather x4, waiting for transfers between devices, gather_rows(): return lax.all_gather(values, 'row', axis=0, tiled=True)  65.9 us
  transfers between devices with their start and end apart: 17, of which 16 were waited for; matrix products, arithmetic and copies ran while one was open for 5% of the time, Pallas kernels for 0%

commit v1 on v0

v1 whole, which is shorter than its diff:
```python
import functools

import jax
import jax.numpy as jnp
from jax import lax
from jax.experimental import pallas as pl
from jax.experimental.pallas import tpu as pltpu
from jax.sharding import PartitionSpec as P

BF = jnp.bfloat16
F32 = jnp.float32
D = 768
WIDE = 384
HD = 64
FF = 3072
FH = 1536
SEQ = 2048
HALF = 1024
TILE = 256
QKV = 3 * WIDE

eps_norm = 1e-05
masked_score = -1e30
LOG2E = 1.4426950408889634


def dot_nn(left, right):
    return lax.dot_general(left, right, (((1,), (0,)), ((), ())), preferred_element_type=F32)


def dot_nt(left, right):
    return lax.dot_general(left, right, (((1,), (1,)), ((), ())), preferred_element_type=F32)


def side_by_side(left, right):
    return jnp.concatenate([left[...], right[...]], 1)


def flip(values, axis, bit=1):
    size = lax.axis_size(axis)
    return lax.ppermute(values, axis, [(i, i ^ bit) for i in range(size)])


def copies(pieces, whole, axis_sizes, sems):
    made = []
    for index, (piece, (row, col)) in enumerate(pieces):
        rows, cols = piece.shape
        target = whole.at[pl.ds(row, rows), pl.ds(col, cols)]
        made.append(pltpu.make_async_copy(piece, target, sems.at[index]))
    return made


def any_spec():
    return pl.BlockSpec(memory_space=pl.ANY)


def project_kernel(spot, own, oth, w_own, w_oth, bias, query, key, value, weight, sems):
    step = pl.program_id(0)

    @pl.when(step == 0)
    def _():
        made = copies([(w_own, (0, 0)), (w_oth, (WIDE, 0))], weight, None, sems)
        for item in made:
            item.start()
        for item in made:
            item.wait()

    rows = side_by_side(own, oth)
    both = dot_nn(rows, weight[:, WIDE:])
    key[...] = both[:, :WIDE].astype(BF)
    value[...] = (both[:, WIDE:] + bias[1:2, :]).astype(BF)

    @pl.when(step // (HALF // TILE) == spot[0])
    def _():
        found = dot_nn(rows, weight[:, :WIDE]) + bias[0:1, :]
        query[...] = (found * (LOG2E * HD ** (-0.5))).astype(BF)


def project(spot, own, oth, w_own, w_oth, bias):
    per = HALF // TILE
    tile = pl.BlockSpec((TILE, WIDE), lambda i, s: (i, 0))
    return pl.pallas_call(
        project_kernel,
        out_shape=(
            jax.ShapeDtypeStruct((HALF, WIDE), BF),
            jax.ShapeDtypeStruct((SEQ, WIDE), BF),
            jax.ShapeDtypeStruct((SEQ, WIDE), BF),
        ),
        grid_spec=pltpu.PrefetchScalarGridSpec(
            num_scalar_prefetch=1,
            grid=(SEQ // TILE,),
            in_specs=[
                tile,
                tile,
                any_spec(),
                any_spec(),
                pl.BlockSpec((8, WIDE), lambda i, s: (0, 0)),
            ],
            out_specs=(
                pl.BlockSpec((TILE, WIDE), lambda i, s: (jnp.clip(i - s[0] * per, 0, per - 1), 0)),
                tile,
                tile,
            ),
            scratch_shapes=[pltpu.VMEM((D, QKV), BF), pltpu.SemaphoreType.DMA((2,))],
        ),
        name="project",
    )(spot, own, oth, w_own, w_oth, bias)


def attend_forward_kernel(pick, live, query, key, value, mixed, logsum, key_s, turned_s):
    pair = pl.program_id(0)
    rows, lanes = query.shape
    lane = lax.broadcasted_iota(jnp.int32, (1, lanes), 1)
    position = lax.broadcasted_iota(jnp.int32, (HALF, 1), 0)
    for head in range(2):
        start = pl.multiple_of(pick[2 * pair + head] * HALF, HALF)
        mine = (lane >= head * HD) & (lane < (head + 1) * HD)
        part = value[pl.ds(start, HALF), :]
        turned_s[head] = jnp.where(mine, part, jnp.ones_like(part)).T
        bias = jnp.where(position + start < live[0], 0.0, masked_score).astype(BF)
        part = key[pl.ds(start, HALF), :]
        other = lane == (1 - head) * HD
        key_s[head] = jnp.where(mine, part, jnp.where(other, bias, jnp.zeros_like(part)))
    query_all = query[...]
    outs = []
    for head in range(2):
        mine = (lane >= head * HD) & (lane < (head + 1) * HD)
        query_head = jnp.where(mine, query_all, jnp.ones_like(query_all))
        scores = dot_nt(key_s[head], query_head)
        top = jnp.max(scores, 0, keepdims=True)
        expo = jnp.exp2(scores - top).astype(BF)
        blend = dot_nn(turned_s[head], expo)
        total = blend[(1 - head) * HD : (1 - head) * HD + 1, :]
        outs.append(blend[head * HD : (head + 1) * HD, :] / total)
        logsum[0, head : head + 1, :] = top + jnp.log2(total)
    mixed[...] = jnp.concatenate(outs, 0).T.astype(BF)


def attend_forward(pick, live, query, key, value):
    rows, width = query.shape
    pairs = width // 128
    return pl.pallas_call(
        attend_forward_kernel,
        out_shape=(
            jax.ShapeDtypeStruct((rows, width), BF),
            jax.ShapeDtypeStruct((pairs, 8, rows), F32),
        ),
        grid_spec=pltpu.PrefetchScalarGridSpec(
            num_scalar_prefetch=2,
            grid=(pairs,),
            in_specs=[
                pl.BlockSpec((rows, 128), lambda p, *_: (0, p)),
                pl.BlockSpec((2 * HALF, 128), lambda p, *_: (0, p)),
                pl.BlockSpec((2 * HALF, 128), lambda p, *_: (0, p)),
            ],
            out_specs=(
                pl.BlockSpec((rows, 128), lambda p, *_: (0, p)),
                pl.BlockSpec((1, 8, rows), lambda p, *_: (p, 0, 0)),
            ),
            scratch_shapes=[pltpu.VMEM((2, HALF, 128), BF), pltpu.VMEM((2, 128, HALF), BF)],
        ),
        name="attend_forward",
    )(pick, live, query, key, value)


def split_three(values):
    high = values.astype(BF)
    rest = values - high.astype(F32)
    middle = rest.astype(BF)
    return high, middle, (rest - middle.astype(F32)).astype(BF)


def attend_backward_kernel(
    pick,
    live,
    query,
    key,
    value,
    mixed,
    grad_mixed,
    logsum,
    grad_query,
    grad_key,
    grad_value,
    query_s,
    grad_s,
):
    pair = pl.program_id(0)
    rows, lanes = query.shape
    lane = lax.broadcasted_iota(jnp.int32, (1, lanes), 1)
    position = lax.broadcasted_iota(jnp.int32, (HALF, 1), 0)
    weighted = mixed[...].astype(F32) * grad_mixed[...].astype(F32)
    sums = logsum[0].T
    grad_key[...] = jnp.zeros_like(grad_key)
    grad_value[...] = jnp.zeros_like(grad_value)
    for head in range(2):
        mine = (lane >= head * HD) & (lane < (head + 1) * HD)
        base = (1 - head) * HD
        delta = jnp.sum(jnp.where(mine, weighted, 0.0), 1, keepdims=True)
        low = jnp.where(mine, grad_mixed[...], jnp.zeros_like(grad_mixed))
        for at, piece in enumerate(split_three(-delta)):
            low = jnp.where(lane == base + at, piece, low)
        grad_s[head] = low
        low = jnp.where(mine, query[...], jnp.zeros_like(query))
        for at, piece in enumerate(split_three(-sums[:, head : head + 1])):
            low = jnp.where(lane == base + at, piece, low)
        query_s[head] = jnp.where(lane == base + 3, jnp.ones_like(low), low)
    turned = jnp.zeros((lanes, rows), F32)
    for head in range(2):
        start = pl.multiple_of(pick[2 * pair + head] * HALF, HALF)
        mine = (lane >= head * HD) & (lane < (head + 1) * HD)
        base = (1 - head) * HD
        extra = (lane >= base) & (lane < base + 3)
        bias = jnp.where(position + start < live[0], 0.0, masked_score).astype(BF)
        key_tile = key[pl.ds(start, HALF), :]
        ones = jnp.ones_like(key_tile)
        zeros = jnp.zeros_like(key_tile)
        fill = jnp.where(extra, ones, jnp.where(lane == base + 3, bias, zeros))
        scores = dot_nt(jnp.where(mine, key_tile, fill), query_s[head])
        value_tile = value[pl.ds(start, HALF), :]
        grad_probs = dot_nt(
            jnp.where(mine, value_tile, jnp.where(extra, ones, zeros)), grad_s[head]
        )
        expo = jnp.exp2(scores)
        grad_scores = (expo * grad_probs).astype(BF)
        found = dot_nn(expo.astype(BF), grad_s[head]).astype(BF)
        grad_value[pl.ds(start, HALF), :] = jnp.where(
            mine, found, grad_value[pl.ds(start, HALF), :]
        )
        found = (dot_nn(grad_scores, query_s[head]) * (1.0 / LOG2E)).astype(BF)
        grad_key[pl.ds(start, HALF), :] = jnp.where(mine, found, grad_key[pl.ds(start, HALF), :])
        turned = turned + dot_nn(jnp.where(mine, key_tile, zeros).T, grad_scores)
    grad_query[...] = (turned * HD ** (-0.5)).T.astype(BF)


def attend_backward(pick, live, query, key, value, mixed, grad_mixed, logsum):
    rows, width = query.shape
    pairs = width // 128
    full = pl.BlockSpec((rows, 128), lambda p, *_: (0, p))
    both = pl.BlockSpec((2 * HALF, 128), lambda p, *_: (0, p))
    return pl.pallas_call(
        attend_backward_kernel,
        out_shape=(
            jax.ShapeDtypeStruct((rows, width), BF),
            jax.ShapeDtypeStruct((2 * HALF, width), BF),
            jax.ShapeDtypeStruct((2 * HALF, width), BF),
        ),
        grid_spec=pltpu.PrefetchScalarGridSpec(
            num_scalar_prefetch=2,
            grid=(pairs,),
            in_specs=[
                full,
                both,
                both,
                full,
                full,
                pl.BlockSpec((1, 8, rows), lambda p, *_: (p, 0, 0)),
            ],
            out_specs=(full, both, both),
            scratch_shapes=[pltpu.VMEM((2, rows, 128), BF), pltpu.VMEM((2, rows, 128), BF)],
        ),
        name="attend_backward",
    )(pick, live, query, key, value, mixed, grad_mixed, logsum)


def gelu_parts(pre):
    bell = jnp.exp2(pre * pre * (-0.5 * LOG2E))
    ratio = 1.0 / (1.0 + jnp.abs(pre) * (0.3275911 * 0.5**0.5))
    tail = 0.5 * 1.061405429 * ratio + 0.5 * -1.453152027
    tail = tail * ratio + 0.5 * 1.421413741
    tail = tail * ratio + 0.5 * -0.284496736
    tail = tail * ratio + 0.5 * 0.254829592
    tail = tail * ratio * bell
    below = jnp.where(pre > 0.0, 1.0 - tail, tail)
    return pre * below, below + pre * bell * 0.3989422804014327


def norm_rows(values):
    centred = values - jnp.mean(values, 1, keepdims=True)
    scale = lax.rsqrt(jnp.mean(centred * centred, 1, keepdims=True) + eps_norm)
    return centred * scale, scale


def norm_back(inner, normal, scale):
    plain = jnp.mean(inner, 1, keepdims=True)
    along = jnp.mean(inner * normal, 1, keepdims=True)
    return scale * (inner - plain - normal * along)


def row_sums(values):
    return jnp.sum(values, 0, keepdims=True)


def chain_forward_kernel(
    spot,
    live,
    mixed_own,
    mixed_oth,
    tok_own,
    tok_oth,
    cot_own,
    cot_oth,
    vectors,
    bias_inter,
    *rest,
):
    pieces = rest[:12]
    (
        out_own,
        out_oth,
        normed_low,
        normal_one,
        scale_one,
        hidden,
        slope,
        grad_two,
        low_own,
        low_oth,
        sums,
    ) = rest[12:23]
    w_attn, w_inter, w_ffout, sems = rest[23:]
    step = pl.program_id(0)
    spots_attn = [(0, 0), (0, WIDE), (WIDE, 0), (WIDE, WIDE)]
    spots_inter = [(0, 0), (WIDE, 0), (0, FH), (WIDE, FH)]
    spots_ffout = [(0, 0), (0, WIDE), (FH, 0), (FH, WIDE)]
    attn_copies = copies(list(zip(pieces[0:4], spots_attn)), w_attn, None, sems.at[0])
    inter_copies = copies(list(zip(pieces[4:8], spots_inter)), w_inter, None, sems.at[1])
    ffout_copies = copies(list(zip(pieces[8:12], spots_ffout)), w_ffout, None, sems.at[2])

    @pl.when(step == 0)
    def _():
        for item in attn_copies + inter_copies + ffout_copies:
            item.start()
        for item in attn_copies:
            item.wait()

    residual = (
        side_by_side(tok_own, tok_oth).astype(F32)
        + dot_nn(side_by_side(mixed_own, mixed_oth), w_attn[...])
        + vectors[0:1, :]
    )
    normal, scale = norm_rows(residual)
    normed = normal * vectors[1:2, :] + vectors[2:3, :]
    low = normed.astype(BF)
    normal_one[...] = normal
    scale_one[...] = jnp.broadcast_to(scale, scale_one.shape)
    normed_low[...] = low

    @pl.when(step == 0)
    def _():
        for item in inter_copies:
            item.wait()

    width = FH // 2
    for part in range(FF // width):
        at = slice(part * width, (part + 1) * width)
        pre = dot_nn(low, w_inter[:, at]) + bias_inter[0:1, at]
        value, factor = gelu_parts(pre)
        hidden[:, at] = value.astype(BF)
        slope[:, at] = factor.astype(BF)

    @pl.when(step == 0)
    def _():
        for item in ffout_copies:
            item.wait()

    residual = normed + dot_nn(hidden[...], w_ffout[...]) + vectors[3:4, :]
    normal, scale = norm_rows(residual)
    layer = (normal * vectors[4:5, :] + vectors[5:6, :]).astype(BF)
    out_own[...] = layer[:, :WIDE]
    out_oth[...] = layer[:, WIDE:]
    rows = lax.broadcasted_iota(jnp.int32, (TILE, 1), 0) + (spot[0] * HALF + step * TILE)
    cot = side_by_side(cot_own, cot_oth).astype(F32)
    cot = jnp.where(rows < live[0], cot, 0.0)
    grad = norm_back(cot * vectors[4:5, :], normal, scale)
    grad_two[...] = grad
    low = grad.astype(BF)
    low_own[...] = low[:, :WIDE]
    low_oth[...] = low[:, WIDE:]

    @pl.when(step == 0)
    def _():
        sums[...] = jnp.zeros_like(sums)

    sums[0:1, :] += row_sums(cot * normal)
    sums[1:2, :] += row_sums(cot)
    sums[2:3, :] += row_sums(grad)


def weight_pieces(weights):
    return [piece for weight in weights for piece in weight]


def chain_forward(spot, live, mixed, tokens, cot, vectors, bias_inter, weights):
    per = HALF // TILE
    row = lambda width: pl.BlockSpec((TILE, width), lambda i, *_: (i, 0))
    mine = pl.BlockSpec((TILE, WIDE), lambda i, s, n: (s[0] * per + i, 0))
    still = lambda rows, width: pl.BlockSpec((rows, width), lambda i, *_: (0, 0))
    shape = lambda width, kind: jax.ShapeDtypeStruct((HALF, width), kind)
    return pl.pallas_call(
        chain_forward_kernel,
        out_shape=(
            shape(WIDE, BF),
            shape(WIDE, BF),
            shape(D, BF),
            shape(D, F32),
            shape(128, F32),
            shape(FF, BF),
            shape(FF, BF),
            shape(D, F32),
            shape(WIDE, BF),
            shape(WIDE, BF),
            jax.ShapeDtypeStruct((8, D), F32),
        ),
        grid_spec=pltpu.PrefetchScalarGridSpec(
            num_scalar_prefetch=2,
            grid=(per,),
            in_specs=[
                row(WIDE),
                row(WIDE),
                mine,
                mine,
                mine,
                row(WIDE),
                still(8, D),
                still(8, FF),
            ]
            + [any_spec()] * 12,
            out_specs=(
                row(WIDE),
                row(WIDE),
                row(D),
                row(D),
                row(128),
                row(FF),
                row(FF),
                row(D),
                row(WIDE),
                row(WIDE),
                still(8, D),
            ),
            scratch_shapes=[
                pltpu.VMEM((D, D), BF),
                pltpu.VMEM((D, FF), BF),
                pltpu.VMEM((FF, D), BF),
                pltpu.SemaphoreType.DMA((3, 4)),
            ],
        ),
        name="chain_forward",
    )(spot, live, *mixed, *tokens, *cot, vectors, bias_inter, *weight_pieces(weights))


def chain_backward_kernel(vectors, grad_two, slope, normal_one, scale_one, *rest):
    pieces = rest[:12]
    (grad_pre, grad_one, low_own, low_oth, mixed_own, mixed_oth, sums, sums_inter) = rest[12:20]
    w_attn, w_inter, w_ffout, sems = rest[20:]
    step = pl.program_id(0)
    spots_attn = [(0, 0), (0, WIDE), (WIDE, 0), (WIDE, WIDE)]
    spots_inter = [(0, 0), (WIDE, 0), (0, FH), (WIDE, FH)]
    spots_ffout = [(0, 0), (0, WIDE), (FH, 0), (FH, WIDE)]
    attn_copies = copies(list(zip(pieces[0:4], spots_attn)), w_attn, None, sems.at[0])
    inter_copies = copies(list(zip(pieces[4:8], spots_inter)), w_inter, None, sems.at[1])
    ffout_copies = copies(list(zip(pieces[8:12], spots_ffout)), w_ffout, None, sems.at[2])

    @pl.when(step == 0)
    def _():
        for item in ffout_copies + inter_copies + attn_copies:
            item.start()
        sums[...] = jnp.zeros_like(sums)
        sums_inter[...] = jnp.zeros_like(sums_inter)
        for item in ffout_copies:
            item.wait()

    low = grad_two[...].astype(BF)
    width = FH // 2
    for part in range(FF // width):
        at = slice(part * width, (part + 1) * width)
        pre = (dot_nt(low, w_ffout[at, :]) * slope[:, at].astype(F32)).astype(BF)
        grad_pre[:, at] = pre
        sums_inter[0:1, at] += row_sums(pre.astype(F32))

    @pl.when(step == 0)
    def _():
        for item in inter_copies:
            item.wait()
        for item in attn_copies:
            item.wait()

    grad = grad_two[...] + dot_nt(grad_pre[...], w_inter[...])
    normal = normal_one[...]
    sums[0:1, :] += row_sums(grad * normal)
    sums[1:2, :] += row_sums(grad)
    grad = norm_back(grad * vectors[1:2, :], normal, scale_one[:, 0:1])
    sums[2:3, :] += row_sums(grad)
    grad_one[...] = grad
    low = grad.astype(BF)
    low_own[...] = low[:, :WIDE]
    low_oth[...] = low[:, WIDE:]
    back = dot_nt(low, w_attn[...]).astype(BF)
    mixed_own[...] = back[:, :WIDE]
    mixed_oth[...] = back[:, WIDE:]


def chain_backward(vectors, grad_two, slope, normal_one, scale_one, weights):
    per = HALF // TILE
    row = lambda width: pl.BlockSpec((TILE, width), lambda i: (i, 0))
    still = lambda rows, width: pl.BlockSpec((rows, width), lambda i: (0, 0))
    shape = lambda width, kind: jax.ShapeDtypeStruct((HALF, width), kind)
    return pl.pallas_call(
        chain_backward_kernel,
        out_shape=(
            shape(FF, BF),
            shape(D, F32),
            shape(WIDE, BF),
            shape(WIDE, BF),
            shape(WIDE, BF),
            shape(WIDE, BF),
            jax.ShapeDtypeStruct((8, D), F32),
            jax.ShapeDtypeStruct((8, FF), F32),
        ),
        grid_spec=pltpu.PrefetchScalarGridSpec(
            num_scalar_prefetch=0,
            grid=(per,),
            in_specs=[still(8, D), row(D), row(FF), row(D), row(128)] + [any_spec()] * 12,
            out_specs=(
                row(FF),
                row(D),
                row(WIDE),
                row(WIDE),
                row(WIDE),
                row(WIDE),
                still(8, D),
                still(8, FF),
            ),
            scratch_shapes=[
                pltpu.VMEM((D, D), BF),
                pltpu.VMEM((D, FF), BF),
                pltpu.VMEM((FF, D), BF),
                pltpu.SemaphoreType.DMA((3, 4)),
            ],
        ),
        name="chain_backward",
    )(vectors, grad_two, slope, normal_one, scale_one, *weight_pieces(weights))


def outer_tall_kernel(left, own, oth, out_own, out_oth):
    found = dot_nn(left[...].T, side_by_side(own, oth))
    out_own[...] = found[:, :WIDE].astype(BF)
    out_oth[...] = found[:, WIDE:].astype(BF)


def outer_tall(left, offset, count, tile, own, oth):
    still = pl.BlockSpec((HALF, WIDE), lambda i: (0, 0))
    made = pl.BlockSpec((tile, WIDE), lambda i: (i, 0))
    shape = jax.ShapeDtypeStruct((count * tile, WIDE), BF)
    return pl.pallas_call(
        outer_tall_kernel,
        out_shape=(shape, shape),
        grid=(count,),
        in_specs=[pl.BlockSpec((HALF, tile), lambda i: (0, offset + i)), still, still],
        out_specs=(made, made),
        name="outer_tall",
    )(left, own, oth)


def outer_wide_kernel(left, right, out_own, out_oth, turned):
    @pl.when(pl.program_id(0) == 0)
    def _():
        turned[...] = left[...].T

    found = dot_nn(turned[...], right[...])
    out_own[...] = found[:WIDE].astype(BF)
    out_oth[...] = found[WIDE:].astype(BF)


def outer_wide(left, right, offset, count, tile):
    made = pl.BlockSpec((WIDE, tile), lambda i: (0, i))
    shape = jax.ShapeDtypeStruct((WIDE, count * tile), BF)
    return pl.pallas_call(
        outer_wide_kernel,
        out_shape=(shape, shape),
        grid=(count,),
        in_specs=[
            pl.BlockSpec((HALF, D), lambda i: (0, 0)),
            pl.BlockSpec((HALF, tile), lambda i: (0, offset + i)),
        ],
        out_specs=(made, made),
        scratch_shapes=[pltpu.VMEM((D, HALF), BF)],
        name="outer_wide",
    )(left, right)


def outer_qkv_kernel(
    spot, tok_own, tok_oth, query, key, value, out_own, out_oth, sums, total
):
    step = pl.program_id(0)
    per = HALF // (2 * TILE)

    @pl.when(step == 0)
    def _():
        total[...] = jnp.zeros_like(total)
        sums[...] = jnp.zeros_like(sums)

    turned = side_by_side(tok_own, tok_oth).T
    total[:, WIDE:] += dot_nn(turned, side_by_side(key, value))
    sums[1:2, :] += row_sums(value[...].astype(F32))

    @pl.when(step // per == spot[0])
    def _():
        total[:, :WIDE] += dot_nn(turned, query[...])
        sums[0:1, :] += row_sums(query[...].astype(F32))

    @pl.when(step == pl.num_programs(0) - 1)
    def _():
        out_own[...] = total[:WIDE].astype(BF)
        out_oth[...] = total[WIDE:].astype(BF)


def outer_qkv(spot, tokens, query, key, value):
    tile = 2 * TILE
    per = HALF // tile
    row = pl.BlockSpec((tile, WIDE), lambda i, s: (i, 0))
    still = pl.BlockSpec((WIDE, QKV), lambda i, s: (0, 0))
    shape = jax.ShapeDtypeStruct((WIDE, QKV), BF)
    return pl.pallas_call(
        outer_qkv_kernel,
        out_shape=(shape, shape, jax.ShapeDtypeStruct((8, WIDE), F32)),
        grid_spec=pltpu.PrefetchScalarGridSpec(
            num_scalar_prefetch=1,
            grid=(SEQ // tile,),
            in_specs=[
                row,
                row,
                pl.BlockSpec((tile, WIDE), lambda i, s: (jnp.clip(i - s[0] * per, 0, per - 1), 0)),
                row,
                row,
            ],
            out_specs=(still, still, pl.BlockSpec((8, WIDE), lambda i, s: (0, 0))),
            scratch_shapes=[pltpu.VMEM((D, QKV), F32)],
        ),
        name="outer_qkv",
    )(spot, *tokens, query, key, value)


def unproject_kernel(
    spot,
    query_own,
    query_oth,
    key_own,
    key_oth,
    value_own,
    value_oth,
    grad_one,
    *rest,
):
    pieces = rest[:4]
    out_own, out_oth, weight, sems = rest[4:]
    step = pl.program_id(0)

    @pl.when(step == 0)
    def _():
        places = [(0, 0), (WIDE, 0), (0, QKV), (WIDE, QKV)]
        made = copies(list(zip(pieces, places)), weight, None, sems)
        for item in made:
            item.start()
        for item in made:
            item.wait()

    own = dot_nt(side_by_side(key_own, value_own), weight[:, WIDE:QKV])
    own = own + dot_nt(side_by_side(key_oth, value_oth), weight[:, QKV + WIDE :])
    here = step // (HALF // TILE) == spot[0]

    @pl.when(here)
    def _():
        found = own + grad_one[...]
        found = found + dot_nt(query_own[...], weight[:, :WIDE])
        found = found + dot_nt(query_oth[...], weight[:, QKV : QKV + WIDE])
        out_own[...] = found[:, :WIDE]
        out_oth[...] = found[:, WIDE:].astype(BF)

    @pl.when(jnp.logical_not(here))
    def _():
        out_own[...] = own[:, :WIDE]
        out_oth[...] = own[:, WIDE:].astype(BF)


def unproject(spot, query, key, value, grad_one, pieces):
    per = HALF // TILE
    row = pl.BlockSpec((TILE, WIDE), lambda i, s: (i, 0))
    clip = lambda i, s: (jnp.clip(i - s[0] * per, 0, per - 1), 0)
    mine = pl.BlockSpec((TILE, WIDE), clip)
    return pl.pallas_call(
        unproject_kernel,
        out_shape=(
            jax.ShapeDtypeStruct((SEQ, WIDE), F32),
            jax.ShapeDtypeStruct((SEQ, WIDE), BF),
        ),
        grid_spec=pltpu.PrefetchScalarGridSpec(
            num_scalar_prefetch=1,
            grid=(SEQ // TILE,),
            in_specs=[mine, mine, row, row, row, row, pl.BlockSpec((TILE, D), clip)]
            + [any_spec()] * 4,
            out_specs=(row, row),
            scratch_shapes=[pltpu.VMEM((D, 2 * QKV), BF), pltpu.SemaphoreType.DMA((4,))],
        ),
        name="unproject",
    )(spot, *query, *key, *value, grad_one, *pieces)


def added(left, right):
    return (left.astype(F32) + right.astype(F32)).astype(BF)


def sum_over_dp(values):
    size = lax.axis_size("dp")
    index = lax.axis_index("dp")
    bits = [1 << k for k in range(size.bit_length() - 1)]
    for bit in bits:
        half = values.shape[0] // 2
        upper = (index & bit) // bit
        send = lax.dynamic_slice_in_dim(values, (1 - upper) * half, half)
        keep = lax.dynamic_slice_in_dim(values, upper * half, half)
        values = added(keep, flip(send, "dp", bit))
    for bit in reversed(bits):
        other = flip(values, "dp", bit)
        upper = (index & bit) != 0
        first = jnp.where(upper, other, values)
        second = jnp.where(upper, values, other)
        values = jnp.concatenate([first, second], 0)
    return values


def sum_everywhere(values):
    for axis in ("row", "col", "dp"):
        for k in range(lax.axis_size(axis).bit_length() - 1):
            values = values + flip(values, axis, 1 << k)
    return values


def in_order(values, index, axis=-1):
    half = values.shape[axis] // 2
    first = lax.slice_in_dim(values, 0, half, axis=axis)
    second = lax.slice_in_dim(values, half, 2 * half, axis=axis)
    swapped = jnp.concatenate([second, first], axis)
    return jnp.where(index == 0, values, swapped)


def padded(rows, width):
    return jnp.concatenate([rows, jnp.zeros((8 - rows.shape[0], width), F32)], 0)


def per_device(
    tokens,
    w_query,
    w_key,
    w_value,
    w_attn_out,
    w_inter,
    w_ffout,
    b_query,
    b_value,
    b_attn_out,
    b_inter,
    b_ffout,
    gain_one,
    shift_one,
    gain_two,
    shift_two,
    lengths,
    block_order,
    cotangent,
):
    row = lax.axis_index("row")
    col = lax.axis_index("col")
    sequence = lax.axis_index("dp") * lax.axis_size("col") + col
    spot = row.reshape(1).astype(jnp.int32)
    live = lax.dynamic_slice(lengths, (sequence,), (1,)).astype(jnp.int32)
    heads = block_order.shape[0] // 2
    picks = lax.dynamic_slice(block_order, (0, row), (2 * heads, 1))[:, 0].astype(jnp.int32)
    picks = in_order(picks, col)

    qkv_0 = jnp.concatenate([w_query.astype(BF), w_key.astype(BF), w_value.astype(BF)], 1)
    qkv_1 = flip(qkv_0, "row")
    tokens_oth = flip(tokens, "row")
    qkv_2 = flip(qkv_0, "col")
    qkv_3 = flip(qkv_2, "row")
    weights = []
    for weight in (w_attn_out, w_inter, w_ffout):
        own = weight.astype(BF)
        over = flip(own, "col")
        weights.append((own, flip(own, "row"), over, flip(over, "row")))
    cot_send = lax.dynamic_slice_in_dim(cotangent, (1 - row) * HALF, HALF)
    cot_oth = flip(cot_send, "row")

    b_query = in_order(b_query, col)
    b_value = in_order(b_value, col)
    qv_bias = [
        padded(jnp.stack([b_query[:WIDE], b_value[:WIDE]]), WIDE),
        padded(jnp.stack([b_query[WIDE:], b_value[WIDE:]]), WIDE),
    ]
    vectors = jnp.stack([b_attn_out, gain_one, shift_one, b_ffout, gain_two, shift_two])
    vectors = padded(in_order(vectors, row), D)
    bias_inter = padded(in_order(b_inter, col)[None], FF)

    both = (tokens, tokens_oth)
    parts = []
    for side, (low, high) in enumerate(((qkv_0, qkv_1), (qkv_2, qkv_3))):
        pick = picks[side * heads : (side + 1) * heads]
        query, key, value = project(spot, *both, low, high, qv_bias[side])
        mixed, logsum = attend_forward(pick, live, query, key, value)
        parts.append((pick, query, key, value, mixed, logsum))

    (
        out_own,
        out_oth,
        normed,
        normal_one,
        scale_one,
        hidden,
        slope,
        grad_two,
        two_own,
        two_oth,
        sums_two,
    ) = chain_forward(
        spot,
        live,
        (parts[0][4], parts[1][4]),
        both,
        (cotangent, cot_oth),
        vectors,
        bias_inter,
        weights,
    )
    out_other = flip(out_oth, "row")
    layer_out = jnp.concatenate(
        [jnp.where(row == 0, out_own, out_other), jnp.where(row == 0, out_other, out_own)], 0
    )

    def over_row(keep, send):
        return added(keep, flip(send, "row"))

    ffout_far = over_row(*outer_tall(hidden, 3, 3, 512, two_own, two_oth))
    ffout_far = flip(ffout_far, "col")
    ffout_near = over_row(*outer_tall(hidden, 0, 3, 512, two_own, two_oth))

    grad_pre, grad_one, one_own, one_oth, mixed_own, mixed_oth, sums_one, sums_inter = (
        chain_backward(vectors, grad_two, slope, normal_one, scale_one, weights)
    )
    inter_far = over_row(*outer_wide(normed, grad_pre, 3, 3, 512))
    attn_far = over_row(*outer_tall(parts[1][4], 0, 1, WIDE, one_own, one_oth))
    wide_far = flip(jnp.concatenate([inter_far, attn_far], 1), "col")
    inter_near = over_row(*outer_wide(normed, grad_pre, 0, 3, 512))
    attn_near = over_row(*outer_tall(parts[0][4], 0, 1, WIDE, one_own, one_oth))

    grad_ffout = sum_over_dp(added(ffout_near, ffout_far))
    grad_wide = sum_over_dp(added(jnp.concatenate([inter_near, attn_near], 1), wide_far))

    grads = [None, None]
    outer = [None, None]
    for side, grad_mixed in ((1, mixed_oth), (0, mixed_own)):
        pick, query, key, value, mixed, logsum = parts[side]
        grads[side] = attend_backward(pick, live, query, key, value, mixed, grad_mixed, logsum)
        keep, send, sums = outer_qkv(spot, both, *grads[side])
        outer[side] = (over_row(keep, send), sums)
    qkv_far = flip(outer[1][0], "col")
    grad_qkv = sum_over_dp(added(outer[0][0], qkv_far))

    near, away = unproject(
        spot,
        (grads[0][0], grads[1][0]),
        (grads[0][1], grads[1][1]),
        (grads[0][2], grads[1][2]),
        grad_one,
        (qkv_0, qkv_1, qkv_2, qkv_3),
    )
    grad_tokens = near + flip(away, "row").astype(F32)

    sums_qv = jnp.concatenate([outer[0][1], outer[1][1]], 1)
    summed = jnp.concatenate(
        [
            in_order(sums_qv[0], col),
            in_order(sums_qv[1], col),
            in_order(sums_one[2], row),
            in_order(sums_inter[0], col),
            in_order(sums_two[2], row),
            in_order(sums_one[0], row),
            in_order(sums_one[1], row),
            in_order(sums_two[0], row),
            in_order(sums_two[1], row),
        ]
    )
    summed = sum_everywhere(summed.reshape(-1, 128)).reshape(-1)
    vector_grads = []
    at = 0
    for width in (D, D, D, FF, D, D, D, D, D):
        vector_grads.append(summed[at : at + width])
        at += width
    grad_qkv = grad_qkv.astype(F32)
    return (
        layer_out,
        grad_tokens,
        grad_qkv[:, :WIDE],
        grad_qkv[:, WIDE : 2 * WIDE],
        grad_qkv[:, 2 * WIDE :],
        grad_wide[:, FH:].astype(F32),
        grad_wide[:, :FH].astype(F32),
        grad_ffout.astype(F32),
        *vector_grads,
    )


def solution(mesh):
    tokens = P(("dp", "col"), "row")
    down = P("row", "col")
    across = P("col", "row")
    return jax.shard_map(
        per_device,
        mesh=mesh,
        in_specs=(tokens, down, down, down, across, down, across) + (P(),) * 11 + (tokens,),
        out_specs=(tokens, tokens, down, down, down, across, down, across) + (P(),) * 9,
        check_vma=False,
    )
```

time: 1200 us -> 514 us (0.43)
  waiting for transfers between devices: 608 us -> 215 us
  matrix products: 291 us -> 0 us
  Pallas kernels: 0 us -> 212 us
  other arithmetic: 148 us -> 22.4 us
  blocking collectives: 58.5 us -> 0 us
  starting transfers between devices: 2.1 us -> 38.1 us
  local copies, waits for them, and re-layouts: 43.4 us -> 15.5 us
  loops' own time: 18.5 us -> 0 us
  between operations: 14.8 us -> 2.08 us
    dot_general x96 -> x0, matrix products: 291 us -> none  [the longest x40 106 us: transposed(): lax.dot_general(left, right, (((1,), (1,)), ((), ())), preferred_element_...]
    reduce_scatter x8 -> x0, waiting for transfers between devices: 274 us -> none  [the longest x4 162 us: sum_cols(): lax.psum_scatter(values.astype(jnp.bfloat16), 'col', scatter_dimension=0,...]
    all_gather x8 -> x0, waiting for transfers between devices: 247 us -> none  [the longest x4 181 us: gather_cols(): return lax.all_gather(values, 'col', axis=0, tiled=True)]
    ppermute x0 -> x50, waiting for transfers between devices: none -> 215 us  [flip(): return lax.ppermute(values, axis, [(i, i ^ bit) for i in range(size)])]
    pallas_call x0 -> x17, Pallas kernels: none -> 212 us  [the longest x2 44.1 us: attend_backward(): pl.pallas_call(attend_backward_kernel, out_shape=(jax.ShapeDtypeStruct((r...]
    psum x1 -> x0, waiting for transfers between devices: 85.6 us -> none  [per_device(): lax.psum(weight_parts[0].astype(jnp.bfloat16), 'dp').astype(jnp.float32)]
    convert_element_type x24 -> x28, other arithmetic: 74.3 us -> 14.1 us  [the longest x3 5.24 us: per_device(): own = weight.astype(BF)]
    psum x5 -> x0, blocking collectives: 58.5 us -> none  [the longest x1 45.2 us: per_device(): lax.psum((vector_parts[0], vector_parts[1], vector_parts[2], vector_parts...]
  transfers between devices with their start and end apart: 17 -> 50, of which waited for: 16 -> 26; matrix products, arithmetic and copies ran while one was open for 5% -> 5% of each run, Pallas kernels for 0% -> 19%
where the time goes in v1:
time: 514 us; the launch traced here: 506 us
  waiting for transfers between devices  215 us (42%)
  Pallas kernels  212 us (41%)
  starting transfers between devices  38.1 us (7%)
  other arithmetic  22.4 us (4%)
  local copies, waits for them, and re-layouts  15.5 us (3%)
    ppermute x50, waiting for transfers between devices, flip(): return lax.ppermute(values, axis, [(i, i ^ bit) for i in range(size)])  215 us
    pallas_call x2, Pallas kernels, attend_backward(): pl.pallas_call(attend_backward_kernel, out_shape=(jax.ShapeDtypeStruct((r...  44.1 us
    ppermute x50, starting transfers between devices, flip(): return lax.ppermute(values, axis, [(i, i ^ bit) for i in range(size)])  38.1 us
    pallas_call x1, Pallas kernels, chain_forward(): pl.pallas_call(chain_forward_kernel, out_shape=(shape(WIDE, BF), shape(WI...  34.7 us
    pallas_call x2, Pallas kernels, attend_forward(): pl.pallas_call(attend_forward_kernel, out_shape=(jax.ShapeDtypeStruct((ro...  24.9 us
    pallas_call x1, Pallas kernels, chain_backward(): pl.pallas_call(chain_backward_kernel, out_shape=(shape(FF, BF), shape(D,...  23.3 us
    pallas_call x2, Pallas kernels, project(): pl.pallas_call(project_kernel, out_shape=(jax.ShapeDtypeStruct((HALF, WID...  21.3 us
    pallas_call x4, Pallas kernels, outer_tall(): pl.pallas_call(outer_tall_kernel, out_shape=(shape, shape), grid=(count,)...  18.9 us
  transfers between devices with their start and end apart: 50, of which 26 were waited for; matrix products, arithmetic and copies ran while one was open for 5% of the time, Pallas kernels for 19%

profile of v1, /device:TPU:0, one launch (start us, length us, event | category | flops | bytes accessed | tf_op | source)
XLA Modules:
  0.0 505.5 jit_solution(17521215229431885807)
XLA Ops:
  16.8 15.0 %collective-permute-done.2.w_own.rest_2_ = bf16[384,1152]{1,0:T(8,128)(2,1)} collective-permute-done((bf16[384,1152]{1,0:T(8,128)(2,1)}, bf16[384,1152]{1,0:T(8,128)(2,1)}, u32[]{:S(2)}, u32[]{:S(2)}) %collective-permute-start.2) | collective-permute-done | bytes 884768 | tf_op jit(solution)/shard_map/ppermute | solution.py:41
  32.4 24.7 %collective-permute-done.9.rest_6_ = bf16[384,1536]{1,0:T(8,128)(2,1)} collective-permute-done((bf16[384,1536]{1,0:T(8,128)(2,1)}, bf16[384,1536]{1,0:T(8,128)(2,1)}, u32[]{:S(2)}, u32[]{:S(2)}) %collective-permute-start.9) | collective-permute-done | bytes 1179680 | tf_op jit(solution)/shard_map/ppermute | solution.py:41
  57.1 24.4 %collective-permute-done.12.rest_10_ = bf16[1536,384]{1,0:T(8,128)(2,1)} collective-permute-done((bf16[1536,384]{1,0:T(8,128)(2,1)}, bf16[1536,384]{1,0:T(8,128)(2,1)}, u32[]{:S(2)}, u32[]{:S(2)}) %collective-permute-start.12) | collective-permute-done | bytes 1179680 | tf_op jit(solution)/shard_map/ppermute | solution.py:41
  88.1 10.6 %project.2 = (bf16[1024,384]{1,0:T(8,128)(2,1)}, bf16[2048,384]{1,0:T(8,128)(2,1)}, bf16[2048,384]{1,0:T(8,128)(2,1)}) custom-call(s32[1]{0:T(128)} %bitcast.spot, bf16[2048,384]{1,0:T(8,128)(2,1)} %tok_own.5, bf16[2048,384]{1,0:T(8,128)(2,1)} %copy-done.1, bf16[384,1152]{1,0:T(8,128)(2,1)} %pad_maximum_fusion.3.w_own.rest_0_, bf16[384,1152]{1,0:T(8,128)(2,1)} %copy-done.3, ...), custom_call_target="tpu_custom_call" | custom-call | tf_op jit(solution)/shard_map/project/pallas_call | solution.py:82
  98.8 12.5 %attend_forward.2 = (bf16[1024,384]{1,0:T(8,128)(2,1)}, f32[3,8,1024]{2,1,0:T(8,128)}) custom-call(s32[6]{0:T(128)} %get-tuple-element.199.pick, s32[1]{0:T(128)} %dynamic_slice.63.live, bf16[1024,384]{1,0:T(8,128)(2,1)} %get-tuple-element.72.query, bf16[2048,384]{1,0:T(8,128)(2,1)} %get-tuple-element.73.key, bf16[2048,384]{1,0:T(8,128)(2,1)} %get-tuple-element.74.value), custom_call_target="tpu_custom_call" | custom-call | tf_op jit(solution)/shard_map/attend_forward/pallas_call | solution.py:142
  111.2 10.7 %project.3 = (bf16[1024,384]{1,0:T(8,128)(2,1)}, bf16[2048,384]{1,0:T(8,128)(2,1)}, bf16[2048,384]{1,0:T(8,128)(2,1)}) custom-call(s32[1]{0:T(128)} %bitcast.spot, bf16[2048,384]{1,0:T(8,128)(2,1)} %tok_own.5, bf16[2048,384]{1,0:T(8,128)(2,1)} %copy-done.1, bf16[384,1152]{1,0:T(8,128)(2,1)} %collective-permute-done.2.w_own.rest_2_, ...), custom_call_target="tpu_custom_call" | custom-call | tf_op jit(solution)/shard_map/project/pallas_call | solution.py:82
  121.9 12.5 %attend_forward.3 = (bf16[1024,384]{1,0:T(8,128)(2,1)}, f32[3,8,1024]{2,1,0:T(8,128)}) custom-call(s32[6]{0:T(128)} %get-tuple-element.198.pick, s32[1]{0:T(128)} %dynamic_slice.63.live, bf16[1024,384]{1,0:T(8,128)(2,1)} %get-tuple-element.76.query, bf16[2048,384]{1,0:T(8,128)(2,1)} %get-tuple-element.77.key, bf16[2048,384]{1,0:T(8,128)(2,1)} %get-tuple-element.78.value), custom_call_target="tpu_custom_call" | custom-call | tf_op jit(solution)/shard_map/attend_forward/pallas_call | solution.py:142
  135.4 34.7 %chain_forward.1 = (bf16[1024,384]{1,0:T(8,128)(2,1)}, bf16[1024,384]{1,0:T(8,128)(2,1)}, bf16[1024,768]{1,0:T(8,128)(2,1)}, f32[1024,768]{1,0:T(8,128)}, f32[10...) custom-call(s32[1]{0:T(128)} %bitcast.spot, ...), custom_call_target="tpu_custom_call" | custom-call | tf_op jit(solution)/shard_map/chain_forward/pallas_call | solution.py:400
  170.2 23.3 %chain_backward.1 = (bf16[1024,3072]{1,0:T(8,128)(2,1)}, f32[1024,768]{1,0:T(8,128)}, bf16[1024,384]{1,0:T(8,128)(2,1)}, bf16[1024,384]{1,0:T(8,128)(2,1)}, bf16...) custom-call(f32[8,768]{1,0:T(8,128)} %concatenate.106.vectors, ...), custom_call_target="tpu_custom_call" | custom-call | tf_op jit(solution)/shard_map/chain_backward/pallas_call | solution.py:509
  193.5 22.0 %attend_backward.2 = (bf16[1024,384]{1,0:T(8,128)(2,1)}, bf16[2048,384]{1,0:T(8,128)(2,1)}, bf16[2048,384]{1,0:T(8,128)(2,1)}) custom-call(s32[6]{0:T(128)} %get-tuple-element.199.pick, s32[1]{0:T(128)} %dynamic_slice.63.live, bf16[1024,384]{1,0:T(8,128)(2,1)} %get-tuple-element.72.query, bf16[2048,384]{1,0:T(8,128)(2,1)} %get-tuple-element.73.key, ...), custom_call_target="tpu_custom_call" | custom-call | tf_op jit(solution)/shard_map/attend_backward/pallas_call | solution.py:241
  215.5 8.2 %outer_qkv.2 = (bf16[384,1152]{1,0:T(8,128)(2,1)}, bf16[384,1152]{1,0:T(8,128)(2,1)}, f32[8,384]{1,0:T(8,128)}) custom-call(s32[1]{0:T(128)} %bitcast.spot, bf16[2048,384]{1,0:T(8,128)(2,1)} %tok_own.5, bf16[2048,384]{1,0:T(8,128)(2,1)} %copy-done.1, bf16[1024,384]{1,0:T(8,128)(2,1)} %get-tuple-element.88.query_own.query, ...), custom_call_target="tpu_custom_call" | custom-call | tf_op jit(solution)/shard_map/outer_qkv/pallas_call | solution.py:625
  227.1 22.1 %attend_backward.3 = (bf16[1024,384]{1,0:T(8,128)(2,1)}, bf16[2048,384]{1,0:T(8,128)(2,1)}, bf16[2048,384]{1,0:T(8,128)(2,1)}) custom-call(s32[6]{0:T(128)} %get-tuple-element.198.pick, s32[1]{0:T(128)} %dynamic_slice.63.live, bf16[1024,384]{1,0:T(8,128)(2,1)} %get-tuple-element.76.query, bf16[2048,384]{1,0:T(8,128)(2,1)} %get-tuple-element.77.key, ...), custom_call_target="tpu_custom_call" | custom-call | tf_op jit(solution)/shard_map/attend_backward/pallas_call | solution.py:241
  249.2 8.2 %outer_qkv.3 = (bf16[384,1152]{1,0:T(8,128)(2,1)}, bf16[384,1152]{1,0:T(8,128)(2,1)}, f32[8,384]{1,0:T(8,128)}) custom-call(s32[1]{0:T(128)} %bitcast.spot, bf16[2048,384]{1,0:T(8,128)(2,1)} %tok_own.5, bf16[2048,384]{1,0:T(8,128)(2,1)} %copy-done.1, bf16[1024,384]{1,0:T(8,128)(2,1)} %get-tuple-element.91.query_oth.query, ...), custom_call_target="tpu_custom_call" | custom-call | tf_op jit(solution)/shard_map/outer_qkv/pallas_call | solution.py:625
  275.8 6.2 %outer_tall.6 = (bf16[1536,384]{1,0:T(8,128)(2,1)}, bf16[1536,384]{1,0:T(8,128)(2,1)}) custom-call(bf16[1024,3072]{1,0:T(8,128)(2,1)} %get-tuple-element.115.left, bf16[1024,384]{1,0:T(8,128)(2,1)} %get-tuple-element.116.own, bf16[1024,384]{1,0:T(8,128)(2,1)} %get-tuple-element.117.oth), custom_call_target="tpu_custom_call" | custom-call | tf_op jit(solution)/shard_map/outer_tall/pallas_call | solution.py:556
  282.0 6.2 %outer_tall.7 = (bf16[1536,384]{1,0:T(8,128)(2,1)}, bf16[1536,384]{1,0:T(8,128)(2,1)}) custom-call(bf16[1024,3072]{1,0:T(8,128)(2,1)} %get-tuple-element.115.left, bf16[1024,384]{1,0:T(8,128)(2,1)} %get-tuple-element.116.own, bf16[1024,384]{1,0:T(8,128)(2,1)} %get-tuple-element.117.oth), custom_call_target="tpu_custom_call" | custom-call | tf_op jit(solution)/shard_map/outer_tall/pallas_call | solution.py:556
  288.2 6.5 %outer_wide.2 = (bf16[384,1536]{1,0:T(8,128)(2,1)}, bf16[384,1536]{1,0:T(8,128)(2,1)}) custom-call(bf16[1024,768]{1,0:T(8,128)(2,1)} %get-tuple-element.103.left, bf16[1024,3072]{1,0:T(8,128)(2,1)} %get-tuple-element.104.right), custom_call_target="tpu_custom_call" | custom-call | tf_op jit(solution)/shard_map/outer_wide/pallas_call | solution.py:579
  294.7 6.6 %outer_wide.3 = (bf16[384,1536]{1,0:T(8,128)(2,1)}, bf16[384,1536]{1,0:T(8,128)(2,1)}) custom-call(bf16[1024,768]{1,0:T(8,128)(2,1)} %get-tuple-element.103.left, bf16[1024,3072]{1,0:T(8,128)(2,1)} %get-tuple-element.104.right), custom_call_target="tpu_custom_call" | custom-call | tf_op jit(solution)/shard_map/outer_wide/pallas_call | solution.py:579
  308.8 15.3 %unproject.1 = (f32[2048,384]{1,0:T(8,128)}, bf16[2048,384]{1,0:T(8,128)(2,1)}) custom-call(s32[1]{0:T(128)} %bitcast.spot, bf16[1024,384]{1,0:T(8,128)(2,1)} %get-tuple-element.88.query_own.query, bf16[1024,384]{1,0:T(8,128)(2,1)} %get-tuple-element.91.query_oth.query, bf16[2048,384]{1,0:T(8,128)(2,1)} %get-tuple-element.92.key_own.key, ...), custom_call_target="tpu_custom_call" | custom-call | tf_op jit(solution)/shard_map/unproject/pallas_call | solution.py:692
  336.6 18.1 %collective-permute-done.18 = bf16[384,1152]{1,0:T(8,128)(2,1)S(1)} collective-permute-done((bf16[384,1152]{1,0:T(8,128)(2,1)S(1)}, bf16[384,1152]{1,0:T(8,128)(2,1)S(1)}, u32[]{:S(2)}, u32[]{:S(2)}) %collective-permute-start.18) | collective-permute-done | bytes 884768 | tf_op jit(solution)/shard_map/ppermute | solution.py:41
  358.6 7.6 %collective-permute-done.19 = bf16[192,1152]{1,0:T(8,128)(2,1)S(1)} collective-permute-done((bf16[192,1152]{1,0:T(8,128)(2,1)S(1)}, bf16[192,1152]{1,0:T(8,128)(2,1)S(1)}, u32[]{:S(2)}, u32[]{:S(2)}) %collective-permute-start.19) | collective-permute-done | bytes 442400 | tf_op jit(solution)/shard_map/ppermute | solution.py:41
  368.0 12.0 %collective-permute-done.38 = bf16[1536,384]{1,0:T(8,128)(2,1)S(1)} collective-permute-done((bf16[1536,384]{1,0:T(8,128)(2,1)S(1)}, bf16[1536,384]{1,0:T(8,128)(2,1)S(1)}, u32[]{:S(2)}, u32[]{:S(2)}) %collective-permute-start.38) | collective-permute-done | bytes 1179680 | tf_op jit(solution)/shard_map/ppermute | solution.py:41
  382.6 5.3 %collective-permute-done.21 = bf16[48,1152]{1,0:T(8,128)(2,1)S(1)} collective-permute-done((bf16[48,1152]{1,0:T(8,128)(2,1)S(1)}, bf16[48,1152]{1,0:T(8,128)(2,1)S(1)}, u32[]{:S(2)}, u32[]{:S(2)}) %collective-permute-start.21) | collective-permute-done | bytes 110624 | tf_op jit(solution)/shard_map/ppermute | solution.py:41
  388.0 23.0 %collective-permute-done.29 = bf16[384,1920]{1,0:T(8,128)(2,1)S(1)} collective-permute-done((bf16[384,1920]{1,0:T(8,128)(2,1)S(1)}, bf16[384,1920]{1,0:T(8,128)(2,1)S(1)}, u32[]{:S(2)}, u32[]{:S(2)}) %collective-permute-start.29) | collective-permute-done | bytes 1474592 | tf_op jit(solution)/shard_map/ppermute | solution.py:41
  415.5 6.1 %collective-permute-done.23 = bf16[96,1152]{1,0:T(8,128)(2,1)S(1)} collective-permute-done((bf16[96,1152]{1,0:T(8,128)(2,1)S(1)}, bf16[96,1152]{1,0:T(8,128)(2,1)S(1)}, u32[]{:S(2)}, u32[]{:S(2)}) %collective-permute-start.23) | collective-permute-done | bytes 221216 | tf_op jit(solution)/shard_map/ppermute | solution.py:41
  426.6 4.3 collective-permute-done.30
  432.8 6.1 %collective-permute-done.24 = bf16[192,1152]{1,0:T(8,128)(2,1)S(1)} collective-permute-done((bf16[192,1152]{1,0:T(8,128)(2,1)S(1)}, bf16[192,1152]{1,0:T(8,128)(2,1)S(1)}, u32[]{:S(2)}, u32[]{:S(2)}) %collective-permute-start.24) | collective-permute-done | bytes 442400 | tf_op jit(solution)/shard_map/ppermute | solution.py:41
  444.0 9.7 %collective-permute-done.32 = bf16[48,1920]{1,0:T(8,128)(2,1)S(1)} collective-permute-done((bf16[48,1920]{1,0:T(8,128)(2,1)S(1)}, bf16[48,1920]{1,0:T(8,128)(2,1)S(1)}, u32[]{:S(2)}, u32[]{:S(2)}) %collective-permute-start.32) | collective-permute-done | bytes 184352 | tf_op jit(solution)/shard_map/ppermute | solution.py:41
  453.9 7.0 %collective-permute-done.42 = bf16[192,384]{1,0:T(8,128)(2,1)S(1)} collective-permute-done((bf16[192,384]{1,0:T(8,128)(2,1)S(1)}, bf16[192,384]{1,0:T(8,128)(2,1)S(1)}, u32[]{:S(2)}, u32[]{:S(2)}) %collective-permute-start.42) | collective-permute-done | bytes 147488 | tf_op jit(solution)/shard_map/ppermute | solution.py:41
  464.9 6.1 %collective-permute-done.43 = bf16[384,384]{1,0:T(8,128)(2,1)S(1)} collective-permute-done((bf16[384,384]{1,0:T(8,128)(2,1)S(1)}, bf16[384,384]{1,0:T(8,128)(2,1)S(1)}, u32[]{:S(2)}, u32[]{:S(2)}) %collective-permute-start.43) | collective-permute-done | bytes 294944 | tf_op jit(solution)/shard_map/ppermute | solution.py:41
  472.1 6.8 %collective-permute-done.34 = bf16[96,1920]{1,0:T(8,128)(2,1)S(1)} collective-permute-done((bf16[96,1920]{1,0:T(8,128)(2,1)S(1)}, bf16[96,1920]{1,0:T(8,128)(2,1)S(1)}, u32[]{:S(2)}, u32[]{:S(2)}) %collective-permute-start.34) | collective-permute-done | bytes 368672 | tf_op jit(solution)/shard_map/ppermute | solution.py:41
  480.9 6.6 %collective-permute-done.44 = bf16[768,384]{1,0:T(8,128)(2,1)S(1)} collective-permute-done((bf16[768,384]{1,0:T(8,128)(2,1)S(1)}, bf16[768,384]{1,0:T(8,128)(2,1)S(1)}, u32[]{:S(2)}, u32[]{:S(2)}) %collective-permute-start.44) | collective-permute-done | bytes 589856 | tf_op jit(solution)/shard_map/ppermute | solution.py:41
  489.3 12.9 %collective-permute-done.35 = bf16[192,1920]{1,0:T(8,128)(2,1)S(1)} collective-permute-done((bf16[192,1920]{1,0:T(8,128)(2,1)S(1)}, bf16[192,1920]{1,0:T(8,128)(2,1)S(1)}, u32[]{:S(2)}, u32[]{:S(2)}) %collective-permute-start.35) | collective-permute-done | bytes 737312 | tf_op jit(solution)/shard_map/ppermute | solution.py:41
  (272 shorter events, 102.2 us)
Async XLA Ops:
  1.9 11.8 %collective-permute-start.6 = (bf16[384,384]{1,0:T(8,128)(2,1)S(1)}, bf16[384,384]{1,0:T(8,128)(2,1)}, u32[]{:S(2)}, u32[]{:S(2)}) collective-permute-start(bf16[384,384]{1,0:T(8,128)(2,1)S(1)} %convert_element_type.216.rest_0_), channel_id=1, source_target_pairs={{0,1},{1,0},{2,3},{3,2},{4,5},{5,4},{6,7},{7,6},{8,9},{9,8},{10,11... | collective-permute-start | bytes 884744 | tf_op jit(solution)/shard_map/ppermute | solution.py:41
  7.3 24.5 %collective-permute-start.2 = (bf16[384,1152]{1,0:T(8,128)(2,1)}, bf16[384,1152]{1,0:T(8,128)(2,1)}, u32[]{:S(2)}, u32[]{:S(2)}) collective-permute-start(bf16[384,1152]{1,0:T(8,128)(2,1)} %pad_maximum_fusion.3.w_own.rest_0_), channel_id=1, source_target_pairs={{0,1},{1,0},{2,3},{3,2},{4,5},{5,4},{6,7},{7,6},{8,9},{9,8},{10,11... | collective-permute-start | bytes 2654216 | tf_op jit(solution)/shard_map/ppermute | solution.py:41
  7.9 73.6 %collective-permute-start = (bf16[2048,384]{1,0:T(8,128)(2,1)S(1)}, bf16[2048,384]{1,0:T(8,128)(2,1)S(1)}, u32[]{:S(2)}, u32[]{:S(2)}) collective-permute-start(bf16[2048,384]{1,0:T(8,128)(2,1)S(1)} %copy-done), channel_id=1, source_target_pairs={{0,2},{2,0},{1,3},{3,1},{4,6},{6,4},{5,7},{7,5},{8,10},{10,8},{9,1... | collective-permute-start | bytes 4718600 | tf_op jit(solution)/shard_map/ppermute | solution.py:41
  9.6 47.5 %collective-permute-start.9 = (bf16[384,1536]{1,0:T(8,128)(2,1)}, bf16[384,1536]{1,0:T(8,128)(2,1)}, u32[]{:S(2)}, u32[]{:S(2)}) collective-permute-start(bf16[384,1536]{1,0:T(8,128)(2,1)} %convert_element_type.217.rest_4_), channel_id=1, source_target_pairs={{0,1},{1,0},{2,3},{3,2},{4,5},{5,4},{6,7},{7,6},{8,9},{9,8},{10,11... | collective-permute-start | bytes 3538952 | tf_op jit(solution)/shard_map/ppermute | solution.py:41
  13.7 67.8 %collective-permute-start.12 = (bf16[1536,384]{1,0:T(8,128)(2,1)}, bf16[1536,384]{1,0:T(8,128)(2,1)}, u32[]{:S(2)}, u32[]{:S(2)}) collective-permute-start(bf16[1536,384]{1,0:T(8,128)(2,1)} %convert_element_type.218.rest_8_), channel_id=1, source_target_pairs={{0,1},{1,0},{2,3},{3,2},{4,5},{5,4},{6,7},{7,6},{8,9},{9,8},{10,11... | collective-permute-start | bytes 3538952 | tf_op jit(solution)/shard_map/ppermute | solution.py:41
  16.7 15.1 %collective-permute-start.1 = (bf16[384,1152]{1,0:T(8,128)(2,1)}, bf16[384,1152]{1,0:T(8,128)(2,1)S(1)}, u32[]{:S(2)}, u32[]{:S(2)}) collective-permute-start(bf16[384,1152]{1,0:T(8,128)(2,1)} %pad_maximum_fusion.3.w_own.rest_0_), channel_id=1, source_target_pairs={{0,2},{2,0},{1,3},{3,1},{4,6},{6,4},{5,7},{7,5},{8,10},{10,8},{9,1... | collective-permute-start | bytes 2654216 | tf_op jit(solution)/shard_map/ppermute | solution.py:41
  31.8 52.5 %collective-permute-start.3 = (bf16[384,1152]{1,0:T(8,128)(2,1)}, bf16[384,1152]{1,0:T(8,128)(2,1)}, u32[]{:S(2)}, u32[]{:S(2)}) collective-permute-start(bf16[384,1152]{1,0:T(8,128)(2,1)} %collective-permute-done.2.w_own.rest_2_), channel_id=1, source_target_pairs={{0,2},{2,0},{1,3},{3,1},{4,6},{6,4},{5,7},{7,5},{8,10},{10,8},{9,1... | collective-permute-start | bytes 2654216 | tf_op jit(solution)/shard_map/ppermute | solution.py:41
  31.8 102.5 %collective-permute-start.11 = (bf16[1536,384]{1,0:T(8,128)(2,1)}, bf16[1536,384]{1,0:T(8,128)(2,1)}, u32[]{:S(2)}, u32[]{:S(2)}) collective-permute-start(bf16[1536,384]{1,0:T(8,128)(2,1)} %convert_element_type.218.rest_8_), channel_id=1, source_target_pairs={{0,2},{2,0},{1,3},{3,1},{4,6},{6,4},{5,7},{7,5},{8,10},{10,8},{9,1... | collective-permute-start | bytes 3538952 | tf_op jit(solution)/shard_map/ppermute | solution.py:41
  57.1 77.3 %collective-permute-start.8 = (bf16[384,1536]{1,0:T(8,128)(2,1)}, bf16[384,1536]{1,0:T(8,128)(2,1)}, u32[]{:S(2)}, u32[]{:S(2)}) collective-permute-start(bf16[384,1536]{1,0:T(8,128)(2,1)} %convert_element_type.217.rest_4_), channel_id=1, source_target_pairs={{0,2},{2,0},{1,3},{3,1},{4,6},{6,4},{5,7},{7,5},{8,10},{10,8},{9,1... | collective-permute-start | bytes 3538952 | tf_op jit(solution)/shard_map/ppermute | solution.py:41
  81.5 52.9 %collective-permute-start.10 = (bf16[384,1536]{1,0:T(8,128)(2,1)}, bf16[384,1536]{1,0:T(8,128)(2,1)}, u32[]{:S(2)}, u32[]{:S(2)}) collective-permute-start(bf16[384,1536]{1,0:T(8,128)(2,1)} %collective-permute-done.9.rest_6_), channel_id=1, source_target_pairs={{0,2},{2,0},{1,3},{3,1},{4,6},{6,4},{5,7},{7,5},{8,10},{10,8},{9,1... | collective-permute-start | bytes 3538952 | tf_op jit(solution)/shard_map/ppermute | solution.py:41
  81.5 52.9 %collective-permute-start.13 = (bf16[1536,384]{1,0:T(8,128)(2,1)}, bf16[1536,384]{1,0:T(8,128)(2,1)S(1)}, u32[]{:S(2)}, u32[]{:S(2)}) collective-permute-start(bf16[1536,384]{1,0:T(8,128)(2,1)} %collective-permute-done.12.rest_10_), channel_id=1, source_target_pairs={{0,2},{2,0},{1,3},{3,1},{4,6},{6,4},{5,7},{7,5},{8,10},{10,8},{9,1... | collective-permute-start | bytes 3538952 | tf_op jit(solution)/shard_map/ppermute | solution.py:41
  84.3 50.1 %collective-permute-start.4 = (bf16[1024,384]{1,0:T(8,128)(2,1)}, bf16[1024,384]{1,0:T(8,128)(2,1)}, u32[]{:S(2)}, u32[]{:S(2)}) collective-permute-start(bf16[1024,384]{1,0:T(8,128)(2,1)} %constant_dynamic-slice_fusion.9), channel_id=1, source_target_pairs={{0,2},{2,0},{1,3},{3,1},{4,6},{6,4},{5,7},{7,5},{8,10},{10,8},{9,1... | collective-permute-start | bytes 2359304 | tf_op jit(solution)/shard_map/ppermute | solution.py:41
  272.9 51.2 %collective-permute-start.49 = (f32[72,128]{1,0:T(8,128)}, f32[72,128]{1,0:T(8,128)}, u32[]{:S(2)}, u32[]{:S(2)}) collective-permute-start(f32[72,128]{1,0:T(8,128)} %add.179), channel_id=1, source_target_pairs={{0,16},{4,20},{8,24},{12,28},{16,0},{20,4},{24,8},{28,12},{1,17},{... | collective-permute-start | bytes 110600 | tf_op jit(solution)/shard_map/ppermute | solution.py:41
  307.8 60.2 %collective-permute-start.36 = (bf16[1536,384]{1,0:T(8,128)(2,1)}, bf16[1536,384]{1,0:T(8,128)(2,1)S(1)}, u32[]{:S(2)}, u32[]{:S(2)}) collective-permute-start(bf16[1536,384]{1,0:T(8,128)(2,1)} %get-tuple-element.119), channel_id=1, source_target_pairs={{0,2},{2,0},{1,3},{3,1},{4,6},{6,4},{5,7},{7,5},{8,10},{10,8},{9,1... | collective-permute-start | bytes 3538952 | tf_op jit(solution)/shard_map/ppermute | solution.py:41
  307.8 22.0 %collective-permute-start.37 = (bf16[1536,384]{1,0:T(8,128)(2,1)}, bf16[1536,384]{1,0:T(8,128)(2,1)S(1)}, u32[]{:S(2)}, u32[]{:S(2)}) collective-permute-start(bf16[1536,384]{1,0:T(8,128)(2,1)} %get-tuple-element.121), channel_id=1, source_target_pairs={{0,2},{2,0},{1,3},{3,1},{4,6},{6,4},{5,7},{7,5},{8,10},{10,8},{9,1... | collective-permute-start | bytes 3538952 | tf_op jit(solution)/shard_map/ppermute | solution.py:41
  308.3 18.1 %collective-permute-start.26 = (bf16[384,384]{1,0:T(8,128)(2,1)}, bf16[384,384]{1,0:T(8,128)(2,1)S(1)}, u32[]{:S(2)}, u32[]{:S(2)}) collective-permute-start(bf16[384,384]{1,0:T(8,128)(2,1)} %get-tuple-element.110), channel_id=1, source_target_pairs={{0,2},{2,0},{1,3},{3,1},{4,6},{6,4},{5,7},{7,5},{8,10},{10,8},{9,1... | collective-permute-start | bytes 884744 | tf_op jit(solution)/shard_map/ppermute | solution.py:41
  308.3 18.5 %collective-permute-start.28 = (bf16[384,384]{1,0:T(8,128)(2,1)}, bf16[384,384]{1,0:T(8,128)(2,1)S(1)}, u32[]{:S(2)}, u32[]{:S(2)}) collective-permute-start(bf16[384,384]{1,0:T(8,128)(2,1)} %get-tuple-element.114), channel_id=1, source_target_pairs={{0,2},{2,0},{1,3},{3,1},{4,6},{6,4},{5,7},{7,5},{8,10},{10,8},{9,1... | collective-permute-start | bytes 884744 | tf_op jit(solution)/shard_map/ppermute | solution.py:41
  330.2 26.5 %collective-permute-start.15 = (bf16[2048,384]{1,0:T(8,128)(2,1)S(1)}, bf16[2048,384]{1,0:T(8,128)(2,1)S(1)}, u32[]{:S(2)}, u32[]{:S(2)}) collective-permute-start(bf16[2048,384]{1,0:T(8,128)(2,1)S(1)} %copy-done.31), channel_id=1, source_target_pairs={{0,2},{2,0},{1,3},{3,1},{4,6},{6,4},{5,7},{7,5},{8,10},{10,8},{9,1... | collective-permute-start | bytes 4718600 | tf_op jit(solution)/shard_map/ppermute | solution.py:41
  332.2 22.5 %collective-permute-start.18 = (bf16[384,1152]{1,0:T(8,128)(2,1)S(1)}, bf16[384,1152]{1,0:T(8,128)(2,1)S(1)}, u32[]{:S(2)}, u32[]{:S(2)}) collective-permute-start(bf16[384,1152]{1,0:T(8,128)(2,1)S(1)} %add_convert_fusion.7), channel_id=1, source_target_pairs={{0,1},{1,0},{2,3},{3,2},{4,5},{5,4},{6,7},{7,6},{8,9},{9,8},{10,11... | collective-permute-start | bytes 2654216 | tf_op jit(solution)/shard_map/ppermute | solution.py:41
  334.1 45.8 %collective-permute-start.38 = (bf16[1536,384]{1,0:T(8,128)(2,1)S(1)}, bf16[1536,384]{1,0:T(8,128)(2,1)S(1)}, u32[]{:S(2)}, u32[]{:S(2)}) collective-permute-start(bf16[1536,384]{1,0:T(8,128)(2,1)S(1)} %add_convert_fusion.2), channel_id=1, source_target_pairs={{0,1},{1,0},{2,3},{3,2},{4,5},{5,4},{6,7},{7,6},{8,9},{9,8},{10,11... | collective-permute-start | bytes 3538952 | tf_op jit(solution)/shard_map/ppermute | solution.py:41
  335.6 75.4 %collective-permute-start.29 = (bf16[384,1920]{1,0:T(8,128)(2,1)S(1)}, bf16[384,1920]{1,0:T(8,128)(2,1)S(1)}, u32[]{:S(2)}, u32[]{:S(2)}) collective-permute-start(bf16[384,1920]{1,0:T(8,128)(2,1)S(1)} %pad_maximum_fusion.1), channel_id=1, source_target_pairs={{0,1},{1,0},{2,3},{3,2},{4,5},{5,4},{6,7},{7,6},{8,9},{9,8},{10,11... | collective-permute-start | bytes 4423688 | tf_op jit(solution)/shard_map/ppermute | solution.py:41
  366.4 14.1 %collective-permute-start.20 = (bf16[96,1152]{1,0:T(8,128)(2,1)S(1)}, bf16[96,1152]{1,0:T(8,128)(2,1)S(1)}, u32[]{:S(2)}, u32[]{:S(2)}) collective-permute-start(bf16[96,1152]{1,0:T(8,128)(2,1)S(1)} %constant_dynamic-slice_fusion.7), channel_id=1, source_target_pairs={{0,8},{4,12},{8,0},{12,4},{16,24},{20,28},{24,16},{28,20},{1,9},{5... | collective-permute-start | bytes 663560 | tf_op jit(solution)/shard_map/ppermute | solution.py:41
  380.8 34.0 %collective-permute-start.39 = (bf16[768,384]{1,0:T(8,128)(2,1)S(1)}, bf16[768,384]{1,0:T(8,128)(2,1)S(1)}, u32[]{:S(2)}, u32[]{:S(2)}) collective-permute-start(bf16[768,384]{1,0:T(8,128)(2,1)S(1)} %constant_dynamic-slice_fusion.2), channel_id=1, source_target_pairs={{0,4},{4,0},{8,12},{12,8},{16,20},{20,16},{24,28},{28,24},{1,5},{5... | collective-permute-start | bytes 1769480 | tf_op jit(solution)/shard_map/ppermute | solution.py:41
  387.9 25.1 %collective-permute-start.22 = (bf16[48,1152]{1,0:T(8,128)(2,1)S(1)}, bf16[48,1152]{1,0:T(8,128)(2,1)S(1)}, u32[]{:S(2)}, u32[]{:S(2)}) collective-permute-start(bf16[48,1152]{1,0:T(8,128)(2,1)S(1)} %add_convert_fusion.19), channel_id=1, source_target_pairs={{0,16},{4,20},{8,24},{12,28},{16,0},{20,4},{24,8},{28,12},{1,17},{... | collective-permute-start | bytes 331784 | tf_op jit(solution)/shard_map/ppermute | solution.py:41
  411.4 19.5 %collective-permute-start.30 = (bf16[192,1920]{1,0:T(8,128)(2,1)S(1)}, bf16[192,1920]{1,0:T(8,128)(2,1)S(1)}, u32[]{:S(2)}, u32[]{:S(2)}) collective-permute-start(bf16[192,1920]{1,0:T(8,128)(2,1)S(1)} %constant_dynamic-slice_fusion.5), channel_id=1, source_target_pairs={{0,4},{4,0},{8,12},{12,8},{16,20},{20,16},{24,28},{28,24},{1,5},{5... | collective-permute-start | bytes 2211848 | tf_op jit(solution)/shard_map/ppermute | solution.py:41
  421.6 17.3 %collective-permute-start.24 = (bf16[192,1152]{1,0:T(8,128)(2,1)S(1)}, bf16[192,1152]{1,0:T(8,128)(2,1)S(1)}, u32[]{:S(2)}, u32[]{:S(2)}) collective-permute-start(bf16[192,1152]{1,0:T(8,128)(2,1)S(1)} %pad_maximum_fusion.6), channel_id=1, source_target_pairs={{0,4},{4,0},{8,12},{12,8},{16,20},{20,16},{24,28},{28,24},{1,5},{5... | collective-permute-start | bytes 1327112 | tf_op jit(solution)/shard_map/ppermute | solution.py:41
  426.2 14.8 %collective-permute-start.41 = (bf16[192,384]{1,0:T(8,128)(2,1)S(1)}, bf16[192,384]{1,0:T(8,128)(2,1)S(1)}, u32[]{:S(2)}, u32[]{:S(2)}) collective-permute-start(bf16[192,384]{1,0:T(8,128)(2,1)S(1)} %constant_dynamic-slice_fusion), channel_id=1, source_target_pairs={{0,16},{4,20},{8,24},{12,28},{16,0},{20,4},{24,8},{28,12},{1,17},{... | collective-permute-start | bytes 442376 | tf_op jit(solution)/shard_map/ppermute | solution.py:41
  440.9 12.9 %collective-permute-start.32 = (bf16[48,1920]{1,0:T(8,128)(2,1)S(1)}, bf16[48,1920]{1,0:T(8,128)(2,1)S(1)}, u32[]{:S(2)}, u32[]{:S(2)}) collective-permute-start(bf16[48,1920]{1,0:T(8,128)(2,1)S(1)} %constant_dynamic-slice_fusion.3), channel_id=1, source_target_pairs={{0,16},{4,20},{8,24},{12,28},{16,0},{20,4},{24,8},{28,12},{1,17},{... | collective-permute-start | bytes 552968 | tf_op jit(solution)/shard_map/ppermute | solution.py:41
  441.0 19.8 %collective-permute-start.42 = (bf16[192,384]{1,0:T(8,128)(2,1)S(1)}, bf16[192,384]{1,0:T(8,128)(2,1)S(1)}, u32[]{:S(2)}, u32[]{:S(2)}) collective-permute-start(bf16[192,384]{1,0:T(8,128)(2,1)S(1)} %add_convert_fusion.18), channel_id=1, source_target_pairs={{0,16},{4,20},{8,24},{12,28},{16,0},{20,4},{24,8},{28,12},{1,17},{... | collective-permute-start | bytes 442376 | tf_op jit(solution)/shard_map/ppermute | solution.py:41
  464.8 14.0 %collective-permute-start.34 = (bf16[96,1920]{1,0:T(8,128)(2,1)S(1)}, bf16[96,1920]{1,0:T(8,128)(2,1)S(1)}, u32[]{:S(2)}, u32[]{:S(2)}) collective-permute-start(bf16[96,1920]{1,0:T(8,128)(2,1)S(1)} %pad_maximum_fusion.7), channel_id=1, source_target_pairs={{0,8},{4,12},{8,0},{12,4},{16,24},{20,28},{24,16},{28,20},{1,9},{5... | collective-permute-start | bytes 1105928 | tf_op jit(solution)/shard_map/ppermute | solution.py:41
  471.3 16.3 %collective-permute-start.44 = (bf16[768,384]{1,0:T(8,128)(2,1)S(1)}, bf16[768,384]{1,0:T(8,128)(2,1)S(1)}, u32[]{:S(2)}, u32[]{:S(2)}) collective-permute-start(bf16[768,384]{1,0:T(8,128)(2,1)S(1)} %pad_maximum_fusion.5), channel_id=1, source_target_pairs={{0,4},{4,0},{8,12},{12,8},{16,20},{20,16},{24,28},{28,24},{1,5},{5... | collective-permute-start | bytes 1769480 | tf_op jit(solution)/shard_map/ppermute | solution.py:41
  479.1 23.2 %collective-permute-start.35 = (bf16[192,1920]{1,0:T(8,128)(2,1)S(1)}, bf16[192,1920]{1,0:T(8,128)(2,1)S(1)}, u32[]{:S(2)}, u32[]{:S(2)}) collective-permute-start(bf16[192,1920]{1,0:T(8,128)(2,1)S(1)} %pad_maximum_fusion.4), channel_id=1, source_target_pairs={{0,4},{4,0},{8,12},{12,8},{16,20},{20,16},{24,28},{28,24},{1,5},{5... | collective-permute-start | bytes 2211848 | tf_op jit(solution)/shard_map/ppermute | solution.py:41
  (53 other events, 589.8 us)
